TPU v7x, 32 devices: a whole 2x2x4 slice. The times are simulated.
32 devices in a mesh: batch: 8 (over z, core), rows: 4 (over y, x).
Axes of the slice: x: 2, y: 2, z: 4, core: 2. Of those that a mesh axis runs over, the one named last changes fastest.
Arguments:
- x_clean: float32 [1024, 3, 16, 16], P('batch', None, 'rows'), may hold values from -1 to 1
- noise: float32 [1024, 3, 16, 16], P('batch', None, 'rows'), may hold values from -5 to 5
- timesteps: int32 [1024], P('batch'), may hold values from 0 to 999
- keep_mask: int32 [1024, 16, 16, 256], P('batch', 'rows'), may hold values 0 or 1
- adam_step: int32 [1], replicated, may hold values from 2 to 20
- inlet_weight: float32 [27, 256], replicated, may hold values from -1.25 to 1.25
- kernel_weight: float32 [2, 2304, 256], replicated, may hold values from -0.125 to 0.125
- attention_weight: float32 [4, 256, 256], replicated, may hold values from -0.375 to 0.375
- time_weight: float32 [640, 512], replicated, may hold values from -0.25 to 0.25
- shift_weight: float32 [512, 256], replicated, may hold values from -0.25 to 0.25
- outlet_weight: float32 [3, 2304], replicated, may hold values from -0.125 to 0.125
- small_params: float32 [19, 256], replicated, may hold values from 0.5 to 1.5
- state_inlet: float32 [2, 27, 256], replicated, as said below
- state_kernel: float32 [2, 2, 2304, 256], P(None, None, 'batch'), as said below
- state_attention: float32 [2, 4, 256, 256], P(None, None, 'batch'), as said below
- state_time: float32 [2, 640, 512], replicated, as said below
- state_shift: float32 [2, 512, 256], replicated, as said below
- state_outlet: float32 [2, 3, 2304], replicated, as said below
- state_small: float32 [2, 19, 256], replicated, as said below
- average_inlet: float32 [27, 256], replicated, may hold values from -1.25 to 1.25
- average_kernel: float32 [2, 2304, 256], P(None, 'batch'), may hold values from -0.125 to 0.125
- average_attention: float32 [4, 256, 256], P(None, 'batch'), may hold values from -0.375 to 0.375
- average_time: float32 [640, 512], replicated, may hold values from -0.25 to 0.25
- average_shift: float32 [512, 256], replicated, may hold values from -0.25 to 0.25
- average_outlet: float32 [3, 2304], replicated, may hold values from -0.125 to 0.125
- average_small: float32 [19, 256], replicated, may hold values from 0.5 to 1.5
Outputs:
- updated_inlet: float32 [2, 27, 256], replicated
- updated_kernel: float32 [2, 2, 2304, 256], replicated
- updated_attention: float32 [2, 4, 256, 256], replicated
- updated_time: float32 [2, 640, 512], replicated
- updated_shift: float32 [2, 512, 256], replicated
- updated_outlet: float32 [2, 3, 2304], replicated
- updated_small: float32 [2, 19, 256], replicated
- first_inlet: float32 [27, 256], replicated
- first_kernel: float32 [2, 2304, 256], P(None, 'batch')
- first_attention: float32 [4, 256, 256], P(None, 'batch')
- first_time: float32 [640, 512], replicated
- first_shift: float32 [512, 256], replicated
- first_outlet: float32 [3, 2304], replicated
- first_small: float32 [19, 256], replicated
- second_inlet: float32 [27, 256], replicated
- second_kernel: float32 [2, 2304, 256], P(None, 'batch')
- second_attention: float32 [4, 256, 256], P(None, 'batch')
- second_time: float32 [640, 512], replicated
- second_shift: float32 [512, 256], replicated
- second_outlet: float32 [3, 2304], replicated
- second_small: float32 [19, 256], replicated
- loss: float32 [], replicated
- gradient_norm: float32 [], replicated
Inputs may be any that keep to these rules, and one draw needn't show every extreme that they name: `state_inlet`: index 0 of each state holds first moments of both signs, index 1 positive second moments. `state_kernel`: as for state_inlet. `state_attention`: as for state_inlet. `state_time`: as for state_inlet. `state_shift`: as for state_inlet. `state_outlet`: as for state_inlet. `state_small`: as for state_inlet.
All inputs are finite; a program needn't handle non-finite values. No bound on the sum of `keep_mask` on one device may be relied on, other than what follows from the above.
Results may differ from a plain program's by a relative error of at most 0.0014.
The roundings to bfloat16 on the way count: a program that leaves them out, or rounds other values in their place, can miss the bound.
Values may be sent and summed in bfloat16 or wider, within the bound.
A program may use at most 640 MiB of HBM per device.

v0:
```python
import functools
import math

import jax
import jax.numpy as jnp
import numpy as np
from jax import lax
from jax.experimental import pallas as pl
from jax.experimental.pallas import tpu as pltpu
from jax.sharding import PartitionSpec as P

G = 32


HIGH_PRECISION = lax.Precision.HIGHEST
CLIP = 0.05
GAMMA = 5.0
KEEP = 0.9
EPS_NORM = 1e-05
BETA_ONE = 0.9
BETA_TWO = 0.999
EPS_ADAM = 1e-08
DECAY = 0.01
EMA_TOP = 0.9999
VMEM_LIMIT = 60 << 20
CHUNK = 8
FORWARD_CHUNK = 4
GROUP = 2
COUNT = 2048.0
RATES = (0.1, 0.01, 0.03, 0.05, 0.02, 0.01, 0.2)


def bar_table():
    beta_rates = 0.0001 + (0.02 - 0.0001) * np.arange(1000, dtype=np.float64) / 999.0
    return np.exp(np.cumsum(np.log(1.0 - beta_rates))).astype(np.float32)


def alpha_bars(timesteps):
    one_hot = (timesteps[:, None] == jnp.arange(1000)[None, :]).astype(jnp.float32)
    return jnp.sum(one_hot * bar_table()[None, :], axis=1)


def sinusoid(timesteps, width):
    half = width // 2
    rates = jnp.exp(-math.log(10000.0) * jnp.arange(half).astype(jnp.float32) / (half - 1))
    angles = timesteps.astype(jnp.float32)[:, None] * rates[None, :]
    return jnp.concatenate([jnp.sin(angles), jnp.cos(angles)], axis=1)


def swish_grad(pre):
    logistic = jax.nn.sigmoid(pre)
    return logistic * (1.0 + pre * (1.0 - logistic))


def wrap(shift, size):
    return shift % size


def tap_masks():
    lane = lax.broadcasted_iota(jnp.int32, (8, 256), 1)
    row, col = lane // 16, lane % 16
    masks = []
    for i in range(3):
        for j in range(3):
            ok = (row + (i - 1) >= 0) & (row + (i - 1) < 16) & (col + (j - 1) >= 0) & (col + (j - 1) < 16)
            masks.append(ok)
    return masks


def tap_stack(tile, masks, sign):
    parts = []
    for tap in range(9):
        step = sign * (16 * (tap // 3 - 1) + tap % 3 - 1)
        moved = tile if step == 0 else pltpu.roll(tile, wrap(-step, 256), 1)
        parts.append(jnp.where(masks[tap if sign > 0 else 8 - tap], moved, 0.0))
    parts.append(jnp.zeros_like(tile))
    return jnp.concatenate(parts, axis=0).astype(jnp.bfloat16)


def group_sum(rows):
    halves = []
    for half in range(2):
        part = rows[:, 128 * half : 128 * half + 128]
        lane = lax.broadcasted_iota(jnp.int32, part.shape, 1)
        for step in (1, 2, 4):
            upper = (lane // step) % 2 == 1
            part = part + jnp.where(upper, pltpu.roll(part, step, 1), pltpu.roll(part, 128 - step, 1))
        halves.append(part)
    return jnp.concatenate(halves, axis=1)


def col_sum(x):
    return jnp.sum(x, axis=0, keepdims=True)


def stats_of(fields):
    sums = jnp.concatenate([col_sum(x) for x in fields] + [col_sum(x * x) for x in fields], axis=0)
    both = group_sum(sums) / COUNT
    n = len(fields)
    mean = both[:n]
    spread = both[n:] - mean * mean
    return mean, lax.rsqrt(spread + EPS_NORM)


def logistic(z):
    return 0.5 * jnp.tanh(0.5 * z) + 0.5


def put_shifted(buf, c, y, not_first, not_last):
    buf[c, 16:272, 256:512] = y.astype(jnp.bfloat16)
    buf[c, 16:272, 0:256] = jnp.where(not_first, pltpu.roll(y, 1, 0), 0.0).astype(jnp.bfloat16)
    buf[c, 16:272, 512:768] = jnp.where(not_last, pltpu.roll(y, 255, 0), 0.0).astype(jnp.bfloat16)


def edge_masks():
    col = lax.broadcasted_iota(jnp.int32, (256, 256), 0) % 16
    return col != 0, col != 15


def stacked(buf, i):
    chunk = buf.shape[0]
    return buf[:, 16 * i : 16 * i + 256, :].reshape(chunk * 256, 768)


def dot(a, b, dims=((1,), (0,))):
    return lax.dot_general(a, b, (dims, ((), ())), preferred_element_type=jnp.float32)


NT = ((1,), (1,))
TN = ((0,), (0,))


def conv_shifted(buf, weight):
    field = jnp.concatenate([stacked(buf, i) for i in range(3)], axis=1)
    return dot(field, weight[...])


def zero_edges(buf):
    edge = jnp.zeros((buf.shape[0], 16, 768), jnp.bfloat16)
    buf[:, 0:16, :] = edge
    buf[:, 272:288, :] = edge


def take_turns(workers):
    live, started = [], 0
    while live or started < len(workers):
        if started < len(workers):
            live.append(workers[started])
            started += 1
        live = [w for w in live if next(w, live) is not live]


def lanes_joined(blocks):
    return blocks[0] if len(blocks) == 1 else jnp.concatenate(blocks, axis=1)


def first_kernel(
    mix, pair, tshift, inlet, kernel_one, small, start_out, inner_out, stats_out, noisy_out, target_out, buf
):
    chunk = start_out.shape[0]
    step = pl.program_id(0)

    @pl.when(step == 0)
    def _():
        zero_edges(buf)

    masks = tap_masks()
    not_first, not_last = edge_masks()
    real = lax.broadcasted_iota(jnp.int32, (8, 256), 0) < 3

    def work(images):
        n = len(images)
        every = range(n)
        low, high = images[0], images[-1] + 1
        starts = []
        for c in images:
            both = lanes_joined([pair[s, c] for s in range(pair.shape[0])])
            clean = jnp.where(real, both, 0.0)
            noise = jnp.where(real, pltpu.roll(both, 5, 0), 0.0)
            noisy = mix[0, step * chunk + c] * clean + mix[1, step * chunk + c] * noise
            noisy = noisy.astype(jnp.bfloat16).astype(jnp.float32)
            noisy_out[c] = noisy
            target_out[c] = noise
            start = dot(tap_stack(noisy, masks, 1), inlet[...], TN) + small[8:9]
            start_out[c] = start
            starts.append(start)
        yield
        mean, rstd = stats_of(starts)
        for i, c in enumerate(images):
            scale = rstd[i : i + 1] * small[0:1]
            z = starts[i] * scale + (small[4:5] - mean[i : i + 1] * scale)
            put_shifted(buf, c, z * logistic(z), not_first, not_last)
        yield
        inner_all = conv_shifted(buf.at[low:high], kernel_one)
        yield
        inners = []
        for i, c in enumerate(images):
            inner = inner_all[256 * i : 256 * i + 256] + tshift[c]
            inner_out[c] = inner
            inners.append(inner)
        mean_two, rstd_two = stats_of(inners)
        for i, c in enumerate(images):
            stats_out[c] = jnp.concatenate(
                [mean[i : i + 1], rstd[i : i + 1], mean_two[i : i + 1], rstd_two[i : i + 1]]
                + [jnp.zeros((4, 256), jnp.float32)],
                axis=0,
            )

    take_turns([work(list(range(g, g + GROUP))) for g in range(0, chunk, GROUP)])


def norm_grad(dys, fields, means, rstds, gain):
    n = len(dys)
    shift_sums, gain_sums = [], []
    for dy, x, mean, rstd in zip(dys, fields, means, rstds):
        shift_sums.append(col_sum(dy))
        gain_sums.append(col_sum(dy * (x * rstd - mean * rstd)))
    both = group_sum(jnp.concatenate(shift_sums + gain_sums, axis=0) * gain) / COUNT
    grads = []
    for c in range(n):
        rstd, mean = rstds[c], means[c]
        slope = -rstd * rstd * both[n + c : n + c + 1]
        base = -rstd * both[c : c + 1] - mean * slope
        grads.append(dys[c] * (rstd * gain) + (fields[c] * slope + base))
    return grads, sum(gain_sums), sum(shift_sums)


def second_kernel(
    tall,
    short,
    coef,
    start_in,
    inner_in,
    stats_in,
    noisy,
    target,
    keep,
    kernel_one_flip,
    kernel_two,
    kernel_two_flip,
    qkv,
    qkv_t,
    proj,
    proj_t,
    outlet,
    small,
    bias_qkv,
    embed,
    hidden,
    hidden_slope,
    time_act,
    time_slope,
    time_two,
    shift_low,
    shard_out,
    rest_out,
    grad_one_out,
    grad_two_out,
    grad_qkv_out,
    grad_proj_out,
    grad_outlet_out,
    grad_inlet_out,
    grad_small_out,
    loss_out,
    tshift_grad,
    buf,
    grad_buf,
):
    chunk = noisy.shape[0]
    step = pl.program_id(0)
    sums = (
        grad_one_out,
        grad_two_out,
        grad_qkv_out,
        grad_proj_out,
        grad_outlet_out,
        grad_inlet_out,
        grad_small_out,
        loss_out,
    )

    @pl.when(step == 0)
    def _():
        zero_edges(buf)
        zero_edges(grad_buf)
        for ref in sums:
            ref[...] = jnp.zeros(ref.shape, jnp.float32)

    masks = tap_masks()
    not_first, not_last = edge_masks()
    scale = 256 ** (-0.5)

    def gain(k):
        return small[k : k + 1]

    def shift(k):
        return small[4 + k : 5 + k]

    def normed(x, mean, rstd, k):
        slope = rstd * gain(k)
        return x * slope + (shift(k) - mean * slope)

    def row(values, c):
        return values[c : c + 1]

    def work(images):
        n = len(images)
        every = range(n)
        low, high = images[0], images[-1] + 1

        def part(x, c):
            return x[256 * c : 256 * c + 256]

        slope_two, act_two = [], []
        for c in images:
            z = normed(inner_in[c], stats_in[c, 2:3], stats_in[c, 3:4], 1)
            s = logistic(z)
            kept = jnp.concatenate([keep[s, c] for s in range(keep.shape[0])], axis=0)
            kept = kept.astype(jnp.float32) * (1.0 / KEEP)
            act = z * s * kept
            slope_two.append(s * (1.0 + z * (1.0 - s)) * kept)
            act_two.append(act.astype(jnp.bfloat16))
            put_shifted(buf, c, act, not_first, not_last)
        yield
        conv_two = conv_shifted(buf.at[low:high], kernel_two)
        yield
        middle = [start_in[c] + part(conv_two, i) + small[10:11] for i, c in enumerate(images)]
        mean, rstd = stats_of(middle)
        mean_three, rstd_three = [row(mean, i) for i in every], [row(rstd, i) for i in every]
        tokens = [
            normed(middle[i], mean_three[i], rstd_three[i], 2).astype(jnp.bfloat16) for i in every
        ]
        tokens = jnp.concatenate(tokens, axis=0)
        yield
        qkv_all = (dot(tokens, qkv[...]) + bias_qkv[0:1]).astype(jnp.bfloat16)
        triples = []
        for i in every:
            three = part(qkv_all, i)
            triples.append((three[:, 0:256], three[:, 256:512], three[:, 512:768]))
        scores = [dot(q, k, NT) for q, k, _ in triples]
        yield
        probs, probs_low = [], []
        for i in every:
            expo = jnp.exp((scores[i] - jnp.max(scores[i], axis=1, keepdims=True)) * scale)
            p = expo * (1.0 / jnp.sum(expo, axis=1, keepdims=True))
            probs.append(p)
            probs_low.append(p.astype(jnp.bfloat16))
        yield
        mixed = [dot(probs_low[i], triples[i][2]).astype(jnp.bfloat16) for i in every]
        mixed = jnp.concatenate(mixed, axis=0)
        branch = dot(mixed, proj[...])
        yield
        final = [middle[i] + part(branch, i) + small[13:14] for i in every]
        mean, rstd = stats_of(final)
        mean_four, rstd_four = [row(mean, i) for i in every], [row(rstd, i) for i in every]
        act_four, slope_four = [], []
        for i in every:
            z = normed(final[i], mean_four[i], rstd_four[i], 3)
            s = logistic(z)
            act_four.append((z * s).astype(jnp.bfloat16))
            slope_four.append(s * (1.0 + z * (1.0 - s)))
        yield
        taps_all = [dot(outlet[...], act, NT) for act in act_four]
        yield
        spreads = []
        loss_sum = 0.0
        for i, c in enumerate(images):
            predicted = 0.0
            for tap in range(9):
                move = 16 * (tap // 3 - 1) + tap % 3 - 1
                moved = taps_all[i][8 * tap : 8 * tap + 8]
                moved = moved if move == 0 else pltpu.roll(moved, wrap(-move, 256), 1)
                predicted = predicted + jnp.where(masks[tap], moved, 0.0)
            error = predicted - target[c]
            weight = coef[step * chunk + c]
            loss_sum = loss_sum + (0.5 * weight) * (error * error)
            grad_pred = (weight * error).astype(jnp.bfloat16).astype(jnp.float32)
            spreads.append(tap_stack(grad_pred, masks, -1))
        loss_out[...] += loss_sum
        yield
        grad_outlet_out[...] += sum(dot(s, act) for s, act in zip(spreads, act_four))
        grad_act = [dot(s, outlet[...], TN) for s in spreads]
        yield
        grad_four = [grad_act[i] * slope_four[i] for i in every]
        grad_final, gain_four, shift_four = norm_grad(grad_four, final, mean_four, rstd_four, gain(3))
        branch_all = jnp.concatenate([g.astype(jnp.bfloat16) for g in grad_final], axis=0)
        yield
        grad_proj_out[...] += dot(mixed, branch_all, TN)
        grad_mixed = dot(branch_all, proj_t[...]).astype(jnp.bfloat16)
        dps = [dot(part(grad_mixed, i), triples[i][2], NT) for i in every]
        dvs = [dot(probs_low[i], part(grad_mixed, i), TN) for i in every]
        yield
        dss = []
        for i in every:
            p, dp = probs[i], dps[i]
            dss.append((p * (dp - jnp.sum(p * dp, axis=1, keepdims=True))).astype(jnp.bfloat16))
        yield
        grad_qkv = []
        for i in every:
            q, k, _ = triples[i]
            dq = dot(dss[i], k) * scale
            dk = dot(dss[i], q, TN) * scale
            grad_qkv.append(jnp.concatenate([dq, dk, dvs[i]], axis=1).astype(jnp.bfloat16))
        grad_qkv_all = jnp.concatenate(grad_qkv, axis=0)
        grad_qkv_out[...] += dot(tokens, grad_qkv_all, TN)
        grad_tokens = dot(grad_qkv_all, qkv_t[...])
        yield
        bias_sums = col_sum(grad_qkv_all.astype(jnp.float32))
        grad_norm, gain_three, shift_three = norm_grad(
            [part(grad_tokens, i) for i in every], middle, mean_three, rstd_three, gain(2)
        )
        grad_middle = [grad_final[i] + grad_norm[i] for i in every]
        for i, c in enumerate(images):
            put_shifted(grad_buf, c, grad_middle[i], not_first, not_last)
        yield
        field = jnp.concatenate(act_two, axis=0)
        for i in range(3):
            grad_two_out[i] += dot(field, stacked(grad_buf.at[low:high], i), TN)
        grad_act = conv_shifted(grad_buf.at[low:high], kernel_two_flip)
        yield
        grad_two = [part(grad_act, i) * slope_two[i] for i in every]
        grad_inner, gain_two, shift_two = norm_grad(
            grad_two,
            [inner_in[c] for c in images],
            [stats_in[c, 2:3] for c in images],
            [stats_in[c, 3:4] for c in images],
            gain(1),
        )
        for i, c in enumerate(images):
            put_shifted(grad_buf, c, grad_inner[i], not_first, not_last)
        act_one, slope_one = [], []
        for c in images:
            z = normed(start_in[c], stats_in[c, 0:1], stats_in[c, 1:2], 0)
            s = logistic(z)
            act_one.append((z * s).astype(jnp.bfloat16))
            slope_one.append(s * (1.0 + z * (1.0 - s)))
        yield
        field = jnp.concatenate(act_one, axis=0)
        for i in range(3):
            grad_one_out[i] += dot(field, stacked(grad_buf.at[low:high], i), TN)
        grad_act = conv_shifted(grad_buf.at[low:high], kernel_one_flip)
        yield
        grad_one = [part(grad_act, i) * slope_one[i] for i in every]
        grad_norm, gain_one, shift_one = norm_grad(
            grad_one,
            [start_in[c] for c in images],
            [stats_in[c, 0:1] for c in images],
            [stats_in[c, 1:2] for c in images],
            gain(0),
        )
        grad_start = [grad_middle[i] + grad_norm[i] for i in every]
        patches = [tap_stack(noisy[c], masks, 1) for c in images]
        inner_sums = [col_sum(g) for g in grad_inner]
        for i, c in enumerate(images):
            tshift_grad[pl.ds(step * chunk + c, 1), :] = inner_sums[i]
        grad_small_out[...] += jnp.concatenate(
            [
                gain_one,
                gain_two,
                gain_three,
                gain_four,
                shift_one,
                shift_two,
                shift_three,
                shift_four,
                sum(col_sum(g) for g in grad_start),
                sum(inner_sums),
                sum(col_sum(g) for g in grad_middle),
                bias_sums[:, 0:256],
                bias_sums[:, 512:768],
                sum(col_sum(g) for g in grad_final),
                jnp.zeros((2, 256), jnp.float32),
            ],
            axis=0,
        )
        yield
        grad_inlet_out[...] += sum(
            dot(patch, g.astype(jnp.bfloat16)) for patch, g in zip(patches, grad_start)
        )

    take_turns([work(list(range(g, g + GROUP))) for g in range(0, chunk, GROUP)])

    @pl.when(step == pl.num_programs(0) - 1)
    def _():
        for k, grad in enumerate((grad_one_out, grad_two_out)):
            for tap in range(9):
                at = 256 * (2 - tap % 3)
                for shard, off, row, size in cuts(tap * 256, 256, tall):
                    shard_out[shard, k * tall + off : k * tall + off + size, :] = grad[
                        2 - tap // 3, row : row + size, at : at + 256
                    ]
        for k in range(4):
            grad, at = (grad_qkv_out, 256 * k) if k < 3 else (grad_proj_out, 0)
            for shard, off, row, size in cuts(0, 256, short):
                low = 2 * tall + k * short + off
                shard_out[shard, low : low + size, :] = grad[row : row + size, at : at + 256]
        used = 2 * tall + 4 * short
        if used < shard_out.shape[1]:
            shard_out[:, used:, :] = jnp.zeros(
                (shard_out.shape[0], shard_out.shape[1] - used, 256), jnp.float32
            )
        total = tshift_grad[...]
        shift_grad = full_dot(time_act[...], total, TN)
        grad_act = full_dot(total, shift_low[...], NT) * time_slope[...]
        two_grad = full_dot(hidden[...], grad_act, TN)
        grad_hidden = full_dot(grad_act, time_two[...], NT) * hidden_slope[...]
        one_grad = full_dot(embed[...], grad_hidden, TN)
        width = one_grad.shape[0]
        height = width + two_grad.shape[0]
        for half in range(2):
            span = slice(256 * half, 256 * half + 256)
            rest_out[half * height : half * height + width, :] = one_grad[:, span]
            rest_out[half * height + width : half * height + height, :] = two_grad[:, span]
        act_sum, hidden_sum = col_sum(grad_act), col_sum(grad_hidden)
        parts = [
            shift_grad,
            grad_inlet_out[...],
            grad_outlet_out[...],
            jnp.concatenate(
                [
                    grad_small_out[0:14],
                    col_sum(total),
                    hidden_sum[:, 0:256],
                    hidden_sum[:, 256:512],
                    act_sum[:, 0:256],
                    act_sum[:, 256:512],
                    jnp.zeros((5, 256), jnp.float32),
                ],
                axis=0,
            ),
            loss_out[...],
        ]
        at = 2 * height
        for part in parts:
            rest_out[at : at + part.shape[0], :] = part
            at += part.shape[0]
        if at < rest_out.shape[0]:
            rest_out[at:, :] = jnp.zeros((rest_out.shape[0] - at, 256), jnp.float32)


def cuts(first, size, height):
    parts, row = [], 0
    while row < size:
        shard, off = divmod(first + row, height)
        take = min(height - off, size - row)
        parts.append((shard, off, row, take))
        row += take
    return parts


def full_dot(a, b, dims):
    return lax.dot_general(
        a.astype(jnp.float32),
        b.astype(jnp.float32),
        (dims, ((), ())),
        precision=HIGH_PRECISION,
        preferred_element_type=jnp.float32,
    )


def resident(shape):
    return pl.BlockSpec(shape, lambda i: (0,) * len(shape), pipeline_mode=pl.Buffered(1))


def per_chunk(chunk, *tail):
    return pl.BlockSpec((chunk,) + tail, lambda i: (i,) + (0,) * len(tail))


def by_source(chunk, block):
    return pl.BlockSpec((block[0], chunk) + block[2:], lambda i: (0, i, 0, 0))


def forward_part(chunk, mix, pair, tshift, inlet, kernel_one, small):
    n = pair.shape[1]
    shapes = [(n, 256, 256), (n, 256, 256), (n, 8, 256), (n, 8, 256), (n, 8, 256)]
    return pl.pallas_call(
        first_kernel,
        grid=(n // chunk,),
        in_specs=[
            pl.BlockSpec(memory_space=pltpu.SMEM),
            by_source(chunk, pair.shape),
            per_chunk(chunk, 1, 256),
            resident(inlet.shape),
            resident(kernel_one.shape),
            resident(small.shape),
        ],
        out_specs=[per_chunk(chunk, *s[1:]) for s in shapes],
        out_shape=[jax.ShapeDtypeStruct(s, jnp.float32) for s in shapes],
        scratch_shapes=[pltpu.VMEM((chunk, 288, 768), jnp.bfloat16)],
        compiler_params=pltpu.CompilerParams(vmem_limit_bytes=VMEM_LIMIT),
        cost_estimate=pl.CostEstimate(
            flops=2 * n * 256 * 256 * 2400, bytes_accessed=n * 1 << 19, transcendentals=n * 1 << 16
        ),
        name="forward_part",
    )(mix, pair, tshift, inlet, kernel_one, small)


def main_part(chunk, sizes, coef, start, inner, stats, noisy, target, keep, weights, small, bias_qkv, times):
    n = noisy.shape[0]
    batch, shard_rows, tall, short, rest_rows = sizes
    outs = [(batch, shard_rows, 256), (rest_rows, 256)]
    sums = [(3, 256, 768), (3, 256, 768), (256, 768), (256, 256), (80, 256), (80, 256), (16, 256), (8, 256)]
    return pl.pallas_call(
        functools.partial(second_kernel, tall, short),
        grid=(n // chunk,),
        in_specs=[
            pl.BlockSpec(memory_space=pltpu.SMEM),
            per_chunk(chunk, 256, 256),
            per_chunk(chunk, 256, 256),
            per_chunk(chunk, 8, 256),
            per_chunk(chunk, 8, 256),
            per_chunk(chunk, 8, 256),
            by_source(chunk, keep.shape),
        ]
        + [resident(w.shape) for w in weights]
        + [resident(small.shape), resident(bias_qkv.shape)]
        + [resident(t.shape) for t in times],
        out_specs=[resident(g) for g in outs],
        out_shape=[jax.ShapeDtypeStruct(g, jnp.float32) for g in outs],
        scratch_shapes=[pltpu.VMEM(g, jnp.float32) for g in sums + [(n, 256)]]
        + [pltpu.VMEM((chunk, 288, 768), jnp.bfloat16)] * 2,
        compiler_params=pltpu.CompilerParams(vmem_limit_bytes=VMEM_LIMIT),
        cost_estimate=pl.CostEstimate(
            flops=70 * n * 2 * 256**3, bytes_accessed=n * 5 << 17, transcendentals=n * 5 << 16
        ),
        name="main_part",
    )(coef, start, inner, stats, noisy, target, keep, *weights, small, bias_qkv, *times)


def rows_first(weight):
    inputs, outputs = weight.shape[0] // 9, weight.shape[1]
    flipped = jnp.transpose(weight.reshape(9, inputs, outputs)[::-1], (0, 2, 1))
    return flipped.reshape(9 * outputs, inputs)


def padded_taps(rows):
    padded = jnp.pad(rows.reshape(9, 3, 256), ((0, 1), (0, 5), (0, 0)))
    return padded.reshape(80, 256)


MESH = pl.DeviceIdType.MESH
MISC_ROWS = (640, 640, 512, 80, 80, 24, 8)
MISC_TOTAL = 2048


def padded_rows(total, parts):
    return -(-total // (8 * parts)) * 8


def exchange_kernel(
    shard_shape,
    rates,
    grads_a,
    grads_b,
    state_kernel,
    state_attention,
    weight_kernel,
    weight_attention,
    scalars,
    out_a,
    out_b,
    shard_grad,
    norm_out,
    half_a,
    half_b,
    row_a,
    row_b,
    deep_a,
    deep_b,
    shard_weight,
    shard_first,
    shard_second,
    square_core,
    square_rows,
    square_deep,
    local_sem,
    core_send,
    core_recv,
    row_send,
    row_recv,
    deep_send,
    deep_recv,
    shard_send,
    shard_recv,
    square_send,
    square_recv,
    deep_send_two,
    deep_recv_two,
    row_send_two,
    row_recv_two,
    core_send_two,
    core_recv_two,
):
    depth, _, rows, piece, _ = grads_a.shape
    lanes = grads_b.shape[3]
    pairs, tall, quads, short = shard_shape
    batch, r = lax.axis_index("batch"), lax.axis_index("rows")
    z, c = batch // 2, batch % 2
    partner = z * 2 + (1 - c)
    row_peers = [(r + d) % rows for d in range(1, rows)]
    deep_peers = [(z + d) % depth for d in range(1, depth)]

    def remote(src, dst, send, recv, where):
        return pltpu.make_async_remote_copy(
            src_ref=src, dst_ref=dst, send_sem=send, recv_sem=recv, device_id=where, device_id_type=MESH
        )

    def blocks(kernel_ref, attention_ref, flat, base, offset):
        copies = []
        for k in range(pairs + quads):
            ref, own, size = (kernel_ref, k, tall) if k < pairs else (attention_ref, k - pairs, short)
            at = k * tall if k < pairs else pairs * tall + own * short
            far = ref.at[own] if offset is None else ref.at[own, pl.ds(offset * size, size)]
            near = flat.at[pl.ds(at, size)]
            copies.append(pltpu.make_async_copy(far, near, local_sem.at[base * (pairs + quads) + k]))
        for copy in copies:
            copy.start()
        return copies

    fetches = (
        blocks(weight_kernel, weight_attention, shard_weight, 0, batch)
        + blocks(state_kernel.at[0], state_attention.at[0], shard_first, 1, None)
        + blocks(state_kernel.at[1], state_attention.at[1], shard_second, 2, None)
    )

    barrier = pltpu.get_barrier_semaphore()
    pl.semaphore_signal(barrier, inc=1, device_id=(partner, r), device_id_type=MESH)
    for peer in row_peers:
        pl.semaphore_signal(barrier, inc=1, device_id=(batch, peer), device_id_type=MESH)
    for peer in deep_peers:
        pl.semaphore_signal(barrier, inc=1, device_id=(peer * 2 + c, r), device_id_type=MESH)
    pl.semaphore_wait(barrier, rows + depth - 1)

    cut = (piece // 8 + 1) // 2 * 8
    chunks = [
        (grads_b, half_b, row_b, deep_b, 0, lanes),
        (grads_a, half_a, row_a, deep_a, 0, cut),
        (grads_a, half_a, row_a, deep_a, cut, piece - cut),
    ]
    pending = []

    core_copies = []
    for k, (grads, half, _, _, at, size) in enumerate(chunks):
        copy = remote(
            grads.at[:, 1 - c, :, pl.ds(at, size)],
            half.at[:, :, pl.ds(at, size)],
            core_send.at[k],
            core_recv.at[k],
            (partner, r),
        )
        copy.start()
        core_copies.append(copy)
    row_copies = []
    for k, (grads, half, row, _, at, size) in enumerate(chunks):
        core_copies[k].wait_recv()

        def add_own(t, carry, grads=grads, half=half, at=at, size=size):
            i, j = t // rows, t % rows
            span = pl.ds(at, size)
            half[i, j, span] = half[i, j, span] + grads[i, c, j, span]
            return carry

        lax.fori_loop(0, depth * rows, add_own, 0)
        copies = []
        for d, peer in enumerate(row_peers):
            copy = remote(
                half.at[:, peer, pl.ds(at, size)],
                row.at[d, :, pl.ds(at, size)],
                row_send.at[k, d],
                row_recv.at[k, d],
                (batch, peer),
            )
            copy.start()
            copies.append(copy)
        row_copies.append(copies)
    deep_copies = []
    for k, (grads, half, row, deep, at, size) in enumerate(chunks):
        for copy in row_copies[k]:
            copy.wait_recv()

        def add_rows(i, carry, half=half, row=row, at=at, size=size):
            span = pl.ds(at, size)
            total = half[i, r, span]
            for d in range(rows - 1):
                total = total + row[d, i, span]
            half[i, r, span] = total
            return carry

        lax.fori_loop(0, depth, add_rows, 0)
        copies = []
        for d, peer in enumerate(deep_peers):
            copy = remote(
                half.at[peer, r, pl.ds(at, size)],
                deep.at[d, pl.ds(at, size)],
                deep_send.at[k, d],
                deep_recv.at[k, d],
                (peer * 2 + c, r),
            )
            copy.start()
            copies.append(copy)
        deep_copies.append(copies)

    def finish(k):
        _, half, _, deep, at, size = chunks[k]
        for copy in deep_copies[k]:
            copy.wait_recv()
        span = pl.ds(at, size)
        total = half[z, r, span]
        for d in range(depth - 1):
            total = total + deep[d, span]
        return total

    def squares(x):
        return jnp.sum((x * x).reshape(-1, 8, 256), axis=0)

    def gather(bufs, k, at, size, stage):
        span = pl.ds(at, size)
        copies = []
        if stage == 0:
            for d, peer in enumerate(deep_peers):
                copies.append(
                    remote(
                        bufs.at[z, c, r, span],
                        bufs.at[z, c, r, span],
                        deep_send_two.at[k, d],
                        deep_recv_two.at[k, d],
                        (peer * 2 + c, r),
                    )
                )
        elif stage == 1:
            for d, peer in enumerate(row_peers):
                copies.append(
                    remote(
                        bufs.at[:, c, r, span],
                        bufs.at[:, c, r, span],
                        row_send_two.at[k, d],
                        row_recv_two.at[k, d],
                        (batch, peer),
                    )
                )
        else:
            copies.append(
                remote(
                    bufs.at[:, c, :, span],
                    bufs.at[:, c, :, span],
                    core_send_two.at[k],
                    core_recv_two.at[k],
                    (partner, r),
                )
            )
        for copy in copies:
            copy.start()
        return copies

    total = finish(0)
    out_b[z, c, r] = total
    stage_zero = [gather(out_b, 0, 0, lanes, 0)]
    line = (batch * rows + r) * lanes + lax.broadcasted_iota(jnp.int32, total.shape, 0)
    square = squares(jnp.where(line < sum(MISC_ROWS[:-1]), total, 0.0))
    for k in (1, 2):
        total = finish(k)
        shard_grad[r, pl.ds(chunks[k][4], chunks[k][5])] = total
        square = square + squares(total)
    square_core[0] = square
    copy = remote(square_core.at[0], square_core.at[1], square_send.at[0], square_recv.at[0], (partner, r))
    copy.start()
    pending.append(copy)
    shard_copies = []
    for d, peer in enumerate(row_peers):
        share = remote(
            shard_grad.at[r], shard_grad.at[r], shard_send.at[d], shard_recv.at[d], (batch, peer)
        )
        share.start()
        shard_copies.append(share)
    copy.wait_recv()
    square_rows[r] = square_core[0] + square_core[1]
    copies = []
    for d, peer in enumerate(row_peers):
        copy = remote(
            square_rows.at[r], square_rows.at[r], square_send.at[1 + d], square_recv.at[1 + d], (batch, peer)
        )
        copy.start()
        copies.append(copy)
    pending += copies
    for copy in copies:
        copy.wait_recv()
    square_deep[z] = sum(square_rows[j] for j in range(rows))
    copies = []
    for d, peer in enumerate(deep_peers):
        copy = remote(
            square_deep.at[z],
            square_deep.at[z],
            square_send.at[rows + d],
            square_recv.at[rows + d],
            (peer * 2 + c, r),
        )
        copy.start()
        copies.append(copy)
    pending += copies
    for copy in copies:
        copy.wait_recv()
    square = sum(square_deep[j] for j in range(depth))
    norm = jnp.sqrt(jnp.sum(jnp.sum(square, axis=0, keepdims=True), axis=1, keepdims=True))
    clip = CLIP / jnp.maximum(norm, CLIP)
    norm_out[...] = jnp.broadcast_to(norm, norm_out.shape)

    def moments(at, g):
        span = pl.ds(at, piece)
        first = BETA_ONE * shard_first[span] + (1.0 - BETA_ONE) * g
        second = BETA_TWO * shard_second[span] + (1.0 - BETA_TWO) * g * g
        return first, second

    for fetch in fetches:
        fetch.wait()
    mine = pl.multiple_of(r * piece, 8)
    first, second = moments(mine, shard_grad[r] * clip)
    line = mine + lax.broadcasted_iota(jnp.int32, first.shape, 0)
    rate = jnp.where(line < pairs * tall, rates[0], rates[1])
    weight = shard_weight[pl.ds(mine, piece)]
    step = first * scalars[0] / (jnp.sqrt(second * scalars[1]) + EPS_ADAM)
    out_a[z, c, r] = weight - rate * (step + DECAY * weight)
    for k in (1, 2):
        stage_zero.append(gather(out_a, k, chunks[k][4], chunks[k][5], 0))
    stage_one, stage_two = [], []
    for k in range(3):
        for copy in stage_zero[k]:
            copy.wait_recv()
        stage_one.append(gather(out_b if k == 0 else out_a, k, chunks[k][4], chunks[k][5], 1))
    for k in range(3):
        for copy in stage_one[k]:
            copy.wait_recv()
        stage_two.append(gather(out_b if k == 0 else out_a, k, chunks[k][4], chunks[k][5], 2))
    for copy in shard_copies:
        copy.wait_recv()
    for copies in stage_two:
        for copy in copies:
            copy.wait_recv()
    pending += core_copies + shard_copies
    for copies in row_copies + deep_copies + stage_zero + stage_one + stage_two:
        pending += copies
    for copy in pending:
        copy.wait_send()


def exchange(grads_a, grads_b, state_kernel, state_attention, weight_kernel, weight_attention, scalars):
    depth, _, rows, piece, width = grads_a.shape
    lanes = grads_b.shape[3]
    pairs, tall = state_kernel.shape[1:3]
    quads, short = state_attention.shape[1:3]
    shape = functools.partial(jax.ShapeDtypeStruct, dtype=jnp.float32)
    whole = pl.BlockSpec(memory_space=pltpu.VMEM)
    dma = pltpu.SemaphoreType.DMA
    vmem = functools.partial(pltpu.VMEM, dtype=jnp.float32)
    return pl.pallas_call(
        functools.partial(exchange_kernel, (pairs, tall, quads, short), (RATES[1], RATES[2])),
        in_specs=[whole] * 2
        + [pl.BlockSpec(memory_space=pl.ANY)] * 4
        + [pl.BlockSpec(memory_space=pltpu.SMEM)],
        out_specs=[whole] * 4,
        out_shape=[
            shape(grads_a.shape),
            shape(grads_b.shape),
            shape((rows, piece, width)),
            shape((8, 128)),
        ],
        scratch_shapes=[
            vmem((depth, rows, piece, width)),
            vmem((depth, rows, lanes, width)),
            vmem((rows - 1, depth, piece, width)),
            vmem((rows - 1, depth, lanes, width)),
            vmem((depth - 1, piece, width)),
            vmem((depth - 1, lanes, width)),
            vmem((rows * piece, width)),
            vmem((rows * piece, width)),
            vmem((rows * piece, width)),
            vmem((2, 8, width)),
            vmem((rows, 8, width)),
            vmem((depth, 8, width)),
            dma((3 * (pairs + quads),)),
            dma((3,)),
            dma((3,)),
            dma((3, rows - 1)),
            dma((3, rows - 1)),
            dma((3, depth - 1)),
            dma((3, depth - 1)),
            dma((rows - 1,)),
            dma((rows - 1,)),
            dma((rows + depth - 1,)),
            dma((rows + depth - 1,)),
            dma((3, depth - 1)),
            dma((3, depth - 1)),
            dma((3, rows - 1)),
            dma((3, rows - 1)),
            dma((3,)),
            dma((3,)),
        ],
        compiler_params=pltpu.CompilerParams(
            collective_id=0, has_side_effects=True, vmem_limit_bytes=VMEM_LIMIT
        ),
        name="exchange",
    )(grads_a, grads_b, state_kernel, state_attention, weight_kernel, weight_attention, scalars)


def finish_kernel(
    scalars,
    norm_tile,
    fresh,
    average_kernel,
    average_attention,
    shard_grad,
    state_kernel,
    state_attention,
    time_left,
    time_right,
    shift_rows,
    rest_rows,
    *refs,
):
    weights, states, averages, refs = refs[:5], refs[5:10], refs[10:15], refs[15:]
    (kernel_out, attention_out), refs = refs[:2], refs[2:]
    updated, firsts, seconds, refs = refs[:5], refs[5:10], refs[10:15], refs[15:]
    first_kernel_out, first_attention_out, second_kernel_out, second_attention_out, loss_out, norm_out = refs
    norm = norm_tile[0:1, 0:1]
    clip = CLIP / jnp.maximum(norm, CLIP)
    kept = scalars[2]

    def averaged(out, index, new, average):
        out[(0,) + index] = new
        out[(1,) + index] = kept * average + (1.0 - kept) * new

    tall, short = state_kernel.shape[2], state_attention.shape[2]
    for k in range(2):
        averaged(kernel_out, (k,), fresh[0, k * tall : k * tall + tall], average_kernel[k])
    for k in range(4):
        at = 2 * tall + k * short
        averaged(attention_out, (k,), fresh[0, at : at + short], average_attention[k])

    def moments(first, second, g):
        return BETA_ONE * first + (1.0 - BETA_ONE) * g, BETA_TWO * second + (1.0 - BETA_TWO) * g * g

    def update(k, rate, grad):
        weight = weights[k][...]
        first, second = moments(states[k][0], states[k][1], grad * clip)
        firsts[k][...] = first
        seconds[k][...] = second
        step = first * scalars[0] / (jnp.sqrt(second * scalars[1]) + EPS_ADAM)
        averaged(updated[k], (), weight - rate * (step + DECAY * weight), averages[k][...])

    update(0, RATES[3], jnp.concatenate([time_left[...], time_right[...]], axis=1))
    update(1, RATES[4], shift_rows[...])

    @pl.when(pl.program_id(0) == 0)
    def _():
        for refs, outs, count, height in (
            (state_kernel, (first_kernel_out, second_kernel_out), 2, tall),
            (state_attention, (first_attention_out, second_attention_out), 4, short),
        ):
            for k in range(count):
                at = k * height + (0 if count == 2 else 2 * tall)
                first, second = moments(refs[0, k], refs[1, k], shard_grad[at : at + height] * clip)
                outs[0][k] = first
                outs[1][k] = second
        inlet = jnp.concatenate([rest_rows[8 * tap : 8 * tap + 3] for tap in range(9)], axis=0)
        outlet = jnp.concatenate([rest_rows[80 + 8 * tap : 83 + 8 * tap] for tap in range(9)], axis=1)
        update(2, RATES[0], inlet)
        update(3, RATES[5], outlet)
        update(4, RATES[6], rest_rows[160:179])
        loss_out[...] = jnp.sum(col_sum(rest_rows[184:192]), axis=1, keepdims=True)
        norm_out[...] = norm


def finish(scalars, norm_tile, fresh, average_kernel, average_attention, shard_grad, state_kernel, state_attention, rest, weights, states, averages):
    batch, shard_rows, width = fresh.shape
    tall, short = state_kernel.shape[2], state_attention.shape[2]
    (time_rows, time_width), (shift_rows, _) = weights[0].shape, weights[1].shape
    time_part, shift_part = time_rows // batch, shift_rows // batch
    shape = functools.partial(jax.ShapeDtypeStruct, dtype=jnp.float32)

    def at(block, index):
        return pl.BlockSpec(block, index)

    def rows_of(k, lead):
        part, wide = ((time_part, time_width), (shift_part, width))[k]
        return pl.BlockSpec(lead + (part, wide), lambda b: (0,) * len(lead) + (b, 0))

    def five(lead):
        return [rows_of(0, lead), rows_of(1, lead)] + [resident(lead + w.shape) for w in weights[2:]]

    shift_at = 2 * time_rows // shift_part
    rest_at = (2 * time_rows + shift_rows) // 256
    return pl.pallas_call(
        finish_kernel,
        grid=(batch,),
        in_specs=[
            pl.BlockSpec(memory_space=pltpu.SMEM),
            resident(norm_tile.shape),
            at((1, shard_rows, width), lambda b: (b, 0, 0)),
            at((2, tall, width), lambda b: (0, b, 0)),
            at((4, short, width), lambda b: (0, b, 0)),
            resident(shard_grad.shape),
            resident(state_kernel.shape),
            resident(state_attention.shape),
            at((time_part, width), lambda b: (b, 0)),
            at((time_part, width), lambda b: (batch + b, 0)),
            at((shift_part, width), lambda b: (shift_at + b, 0)),
            pl.BlockSpec((256, width), lambda b: (rest_at, 0), pipeline_mode=pl.Buffered(1)),
        ]
        + five(())
        + five((2,))
        + five(()),
        out_specs=[
            at((2, 2, tall, width), lambda b: (0, 0, b, 0)),
            at((2, 4, short, width), lambda b: (0, 0, b, 0)),
        ]
        + five((2,))
        + five(())
        + five(())
        + [resident(state_kernel.shape[1:]), resident(state_attention.shape[1:])] * 2
        + [resident((1, 1))] * 2,
        out_shape=[
            shape((2, 2, batch * tall, width)),
            shape((2, 4, batch * short, width)),
        ]
        + [shape((2,) + w.shape) for w in weights]
        + [shape(w.shape) for w in weights] * 2
        + [shape(state_kernel.shape[1:]), shape(state_attention.shape[1:])] * 2
        + [shape((1, 1))] * 2,
        compiler_params=pltpu.CompilerParams(vmem_limit_bytes=VMEM_LIMIT),
        cost_estimate=pl.CostEstimate(flops=40 << 20, bytes_accessed=36 << 20, transcendentals=1 << 20),
        name="finish",
    )(
        scalars,
        norm_tile,
        fresh,
        average_kernel,
        average_attention,
        shard_grad,
        state_kernel,
        state_attention,
        rest,
        rest,
        rest,
        rest,
        *weights,
        *states,
        *averages,
    )


def local(
    x_clean,
    noise,
    timesteps,
    keep_mask,
    adam_step,
    inlet_weight,
    kernel_weight,
    attention_weight,
    time_weight,
    shift_weight,
    outlet_weight,
    small_params,
    state_inlet,
    state_kernel,
    state_attention,
    state_time,
    state_shift,
    state_outlet,
    state_small,
    average_inlet,
    average_kernel,
    average_attention,
    average_time,
    average_shift,
    average_outlet,
    average_small,
):
    chans = kernel_weight.shape[2]
    width_sin = time_weight.shape[0] - time_weight.shape[1]
    rows, batch = lax.axis_size("rows"), lax.axis_size("batch")
    own = timesteps.shape[0] // rows
    pair = jnp.concatenate([x_clean, noise], axis=1)
    pair = pair.reshape(rows, own, 6, -1)
    pair = jnp.pad(pair, ((0, 0), (0, 0), (0, 2), (0, 0)))
    pair = lax.all_to_all(pair, "rows", 0, 0, tiled=True)
    keep = keep_mask.reshape(rows, own, -1, chans).astype(jnp.bfloat16)
    (
        keep,
        timesteps,
        adam_step,
        inlet_low,
        kernels,
        projections,
        time_low,
        shift_low,
        outlet_low,
        small_low,
    ) = lax.optimization_barrier(
        (
            keep,
            timesteps,
            adam_step,
            inlet_weight,
            kernel_weight,
            attention_weight,
            time_weight,
            shift_weight,
            outlet_weight,
            small_params,
        )
    )
    keep = lax.all_to_all(keep, "rows", 0, 0, tiled=True)
    timesteps = lax.dynamic_slice_in_dim(timesteps, lax.axis_index("rows") * own, own, 0)
    bars = alpha_bars(timesteps)
    mix = jnp.stack([jnp.sqrt(bars), jnp.sqrt(1.0 - bars)])
    kernels = kernels.astype(jnp.bfloat16)
    projections = projections.astype(jnp.bfloat16)
    time_low = time_low.astype(jnp.bfloat16)
    shift_low = shift_low.astype(jnp.bfloat16)
    inlet = padded_taps(inlet_low).astype(jnp.bfloat16)
    outlet = padded_taps(
        jnp.transpose(outlet_low.reshape(3, 9, chans), (1, 0, 2)).reshape(27, chans)
    ).astype(jnp.bfloat16)
    qkv = jnp.concatenate([projections[0], projections[1], projections[2]], axis=1)
    embed = sinusoid(timesteps, width_sin).astype(jnp.bfloat16)
    hidden_pre = jnp.dot(
        embed, time_low[:width_sin], preferred_element_type=jnp.float32
    ) + small_low[15:17].reshape(-1)
    hidden = jax.nn.silu(hidden_pre).astype(jnp.bfloat16)
    time_emb = jnp.dot(
        hidden, time_low[width_sin:], preferred_element_type=jnp.float32
    ) + small_low[17:19].reshape(-1)
    time_act = jax.nn.silu(time_emb).astype(jnp.bfloat16)
    time_shift = jnp.dot(time_act, shift_low, preferred_element_type=jnp.float32) + small_low[14]
    ratio = bars / (1.0 - bars)
    snr_weight = jnp.minimum(ratio, GAMMA) / ratio
    denom = 3 * 256 * own * rows * batch
    coef = 2.0 * snr_weight / denom
    start, inner, stats, noisy, target = forward_part(
        FORWARD_CHUNK, mix, pair, (time_shift + small_low[9])[:, None, :], inlet, kernels[0], small_low
    )
    bias_qkv = jnp.concatenate([small_low[11], jnp.zeros_like(small_low[0]), small_low[12]])
    tall, short = state_kernel.shape[2], state_attention.shape[2]
    shard_rows = rows * padded_rows(2 * tall + 4 * short, rows)
    lanes = padded_rows(MISC_TOTAL, batch * rows)
    shards, rest = main_part(
        CHUNK,
        (batch, shard_rows, tall, short, batch * rows * lanes),
        coef,
        start,
        inner,
        stats,
        noisy,
        target,
        keep,
        (
            rows_first(kernels[0]),
            kernels[1],
            rows_first(kernels[1]),
            qkv,
            qkv.T,
            projections[3],
            projections[3].T,
            outlet,
        ),
        small_low,
        bias_qkv[None],
        (
            embed,
            hidden,
            swish_grad(hidden_pre),
            time_act,
            swish_grad(time_emb),
            time_low[width_sin:],
            shift_low,
        ),
    )
    count = adam_step[0].astype(jnp.float32)
    scalars = jnp.stack(
        [
            1.0 / (1.0 - BETA_ONE**count),
            1.0 / (1.0 - BETA_TWO**count),
            jnp.minimum(EMA_TOP, (1.0 + count) / (10.0 + count)),
        ]
    )
    fresh, rest, shard_grad, norm_tile = exchange(
        shards.reshape(batch // 2, 2, rows, shard_rows // rows, chans),
        rest.reshape(batch // 2, 2, rows, lanes, chans),
        state_kernel,
        state_attention,
        kernel_weight,
        attention_weight,
        scalars,
    )
    results = finish(
        scalars,
        norm_tile,
        fresh.reshape(batch, shard_rows, chans),
        lax.all_gather(average_kernel, "batch", axis=1, tiled=True),
        lax.all_gather(average_attention, "batch", axis=1, tiled=True),
        shard_grad.reshape(shard_rows, chans),
        state_kernel,
        state_attention,
        rest.reshape(-1, chans),
        (time_weight, shift_weight, inlet_weight, outlet_weight, small_params),
        (state_time, state_shift, state_inlet, state_outlet, state_small),
        (average_time, average_shift, average_inlet, average_outlet, average_small),
    )
    kernel_pair, attention_pair = results[:2]
    triples = [results[2 + 5 * k : 7 + 5 * k] for k in range(3)]
    first_conv, first_attention, second_conv, second_attention, loss, norm = results[17:]
    ordered = []
    for (time, shift, inlet, outlet, small), middle in zip(
        triples,
        ((kernel_pair, attention_pair), (first_conv, first_attention), (second_conv, second_attention)),
    ):
        ordered += [inlet, *middle, time, shift, outlet, small]
    return (*ordered, loss.reshape(()), norm.reshape(()))


def solution(mesh):
    return jax.shard_map(
        local,
        mesh=mesh,
        in_specs=(
            P("batch", None, "rows", None),
            P("batch", None, "rows", None),
            P("batch"),
            P("batch", "rows", None, None),
            P(),
            P(),
            P(),
            P(),
            P(),
            P(),
            P(),
            P(),
            P(),
            P(None, None, "batch", None),
            P(None, None, "batch", None),
            P(),
            P(),
            P(),
            P(),
            P(),
            P(None, "batch", None),
            P(None, "batch", None),
            P(),
            P(),
            P(),
            P(),
        ),
        out_specs=(
            P(),
            P(),
            P(),
            P(),
            P(),
            P(),
            P(),
            P(),
            P(None, "batch", None),
            P(None, "batch", None),
            P(),
            P(),
            P(),
            P(),
            P(),
            P(None, "batch", None),
            P(None, "batch", None),
            P(),
            P(),
            P(),
            P(),
            P(),
            P(),
        ),
        check_vma=False,
    )
```

profile of v0, /device:TPU:1, one launch (start us, length us, event | category | flops | bytes accessed | tf_op | source)
XLA Modules:
  0.0 378.8 jit_solution(6402425400230831533)
XLA Ops:
  7.9 1.0 pad_maximum_fusion.1
  9.7 1.0 reshape.156
  10.7 4.3 %all-to-all-start = ((f32[4,1,16384]{2,1,0:T(1,128)}), f32[4,1,16384]{2,1,0:T(1,128)}, u32[]{:S(2)}, u32[]{:S(2)}) async-start(f32[4,1,16384]{2,1,0:T(1,128)} %reshape.156), calls=%async_computation | async-start | bytes 524288 | tf_op jit(solution)/shard_map/all_to_all | solution.py:1185
  15.0 0.7 all-gather.3.cloned.1.call-update
  15.7 6.8 %convert_element_type.51 = bf16[128,4,16,256]{3,2,1,0:T(8,128)(2,1)} convert(s32[128,4,16,256]{3,2,1,0:T(8,128)} %param.30) | non-fusion elementwise | flops 2097152 | bytes 12582912 | tf_op jit(solution)/shard_map/convert_element_type | solution.py:1186
  22.6 0.8 slice_bitcast_fusion.5
  23.4 1.4 fusion.9
  26.0 0.9 convert_element_type.56
  27.5 0.7 convert_element_type.59.shift_low
  28.3 2.7 convert_element_type.61
  31.0 1.0 copy.79
  32.0 1.8 slice_bitcast_fusion.3
  35.1 4.8 %all-to-all-start.1 = ((bf16[4,32,64,256]{3,2,1,0:T(8,128)(2,1)}), bf16[4,32,64,256]{3,2,1,0:T(8,128)(2,1)}, u32[]{:S(2)}, u32[]{:S(2)}) async-start(bf16[4,32,64,256]{3,2,1,0:T(8,128)(2,1)} %bitcast.64), calls=%async_computation.1 | async-start | bytes 8388608 | tf_op jit(solution)/shard_map/all_to_all | solution.py:1212
  40.6 0.9 fusion.6
  41.5 1.7 fusion.8
  43.4 0.9 copy-done.2
  44.3 0.8 add_multiply_fusion.1
  45.1 0.9 add_multiply_fusion
  47.2 0.8 slice.61.time_two
  49.3 0.9 copy.81.qkv
  50.8 0.8 copy.82.proj
  52.3 1.1 rev.7
  53.4 1.5 copy.77
  58.7 2.3 reduce
  61.0 1.1 reshape.157.pair
  62.1 25.7 %forward_part.1 = (f32[32,256,256]{2,1,0:T(8,128)}, f32[32,256,256]{2,1,0:T(8,128)}, f32[32,8,256]{2,1,0:T(8,128)}, f32[32,8,256]{2,1,0:T(8,128)}, f32[32,8,256]{2,1,0:T(8,128)}) custom-call(f32[2,32]{1,0:T(2,128)} %pad_maximum_fusion.4.mix, f32[4,32,8,64]{3,2,1,0:T(8,128)} %reshape.157.pair, f32[32,1,256]{2,1,0:T(1,128)} %broadcast_in_dim.6.tshift, ...), custom_call_target="tpu_custom_call" | custom-call | flops 10066329600 | bytes 16777216 | tf_op jit(solution)/shard_map/forward_part/pallas_call | solution.py:576
  87.8 130.6 %main_part.1 = (f32[8,704,256]{2,1,0:T(8,128)}, f32[2048,256]{1,0:T(8,128)}) custom-call(f32[32]{0:T(128)} %get-tuple-element.206.coef, f32[32,256,256]{2,1,0:T(8,128)} %get-tuple-element.74.start_in, f32[32,256,256]{2,1,0:T(8,128)} %get-tuple-element.75.inner_in, f32[32,8,256]{2,1,0:T(8,128)} %get-tuple-element.76.stats_in, ...), custom_call_target="tpu_custom_call" | custom-call | flops 75161927680 | bytes 20971520 | tf_op jit(solution)/shard_map/main_part/pallas_call | solution.py:603
  218.4 130.8 %exchange.1 = (f32[4,2,4,176,256]{4,3,2,1,0:T(8,128)}, f32[4,2,4,64,256]{4,3,2,1,0:T(8,128)}, f32[4,176,256]{2,1,0:T(8,128)}, f32[8,128]{1,0:T(8,128)}) custom-call(f32[4,2,4,176,256]{4,3,2,1,0:T(8,128)} %bitcast.65, f32[4,2,4,64,256]{4,3,2,1,0:T(8,128)} %bitcast.69, f32[2,2,288,256]{3,2,1,0:T(8,128)} %state_kernel.3, f32[2,4,32,256]{3,2,1,0:T(8,128)} %state_attention.3, ...), custom_call_target="tpu_custom_call" | custom-call | tf_op jit(solution)/shard_map/exchange/pallas_call | solution.py:954
  349.3 17.8 %finish.1 = (f32[2,2,2304,256]{3,2,1,0:T(8,128)}, f32[2,4,256,256]{3,2,1,0:T(8,128)}, f32[2,640,512]{2,1,0:T(8,128)}, f32[2,512,256]{2,1,0:T(8,128)}, f32[2,27,2...) custom-call(f32[3]{0:T(128)} %pad_maximum_fusion.5.scalars, ...), custom_call_target="tpu_custom_call" | custom-call | flops 41943040 | bytes 37748736 | tf_op jit(solution)/shard_map/finish/pallas_call | solution.py:1091
  367.1 1.5 copy.86
  368.6 1.5 copy.87
  370.1 1.4 copy.88
  (79 shorter events, 11.9 us)
Async XLA Ops:
  7.2 342.0 %all-gather.5.cloned.1.call-start = ((), (), s32[]{:S(2)}) async-start(), calls=%async_computation.3 | async-start | bytes 1179648 | tf_op jit(solution)/shard_map/all_gather | solution.py:1300
  10.7 24.4 %all-to-all-start = ((f32[4,1,16384]{2,1,0:T(1,128)}), f32[4,1,16384]{2,1,0:T(1,128)}, u32[]{:S(2)}, u32[]{:S(2)}) async-start(f32[4,1,16384]{2,1,0:T(1,128)} %reshape.156), calls=%async_computation | async-start | bytes 524288 | tf_op jit(solution)/shard_map/all_to_all | solution.py:1185
  15.0 334.3 %all-gather.3.cloned.1.call-start = ((), (), s32[]{:S(2)}) async-start(), calls=%async_computation.2 | async-start | bytes 5308416 | tf_op jit(solution)/shard_map/all_gather | solution.py:1299
  15.7 10.3 %copy-start = (f32[640,512]{1,0:T(8,128)S(1)}, f32[640,512]{1,0:T(8,128)}, u32[]{:S(2)}) copy-start(f32[640,512]{1,0:T(8,128)} %refs_0_.1) | copy-start | bytes 3932164
  22.6 5.0 %copy-start.3 = (f32[512,256]{1,0:T(8,128)S(1)}, f32[512,256]{1,0:T(8,128)}, u32[]{:S(2)}) copy-start(f32[512,256]{1,0:T(8,128)} %refs_1_.1) | copy-start | bytes 1572868
  28.3 2.7 copy-start.1
  31.0 3.0 copy-start.19
  31.0 3.3 copy-start.16
  34.3 9.0 %copy-start.14 = (bf16[32,128]{1,0:T(8,128)(2,1)}, bf16[32,128]{1,0:T(8,128)(2,1)S(1)}, u32[]{:S(2)}) copy-start(bf16[32,128]{1,0:T(8,128)(2,1)S(1)} %pad_maximum_fusion.2.embed) | copy-start | bytes 24580
  35.1 52.7 %all-to-all-start.1 = ((bf16[4,32,64,256]{3,2,1,0:T(8,128)(2,1)}), bf16[4,32,64,256]{3,2,1,0:T(8,128)(2,1)}, u32[]{:S(2)}, u32[]{:S(2)}) async-start(bf16[4,32,64,256]{3,2,1,0:T(8,128)(2,1)} %bitcast.64), calls=%async_computation.1 | async-start | bytes 8388608 | tf_op jit(solution)/shard_map/all_to_all | solution.py:1212
  43.2 1.1 copy-start.2
  43.2 1.1 copy-start.17
  43.2 1.9 copy-start.18
  43.2 2.8 copy-start.5
  43.2 2.8 copy-start.15
  43.2 5.4 %copy-start.8 = (f32[27,256]{1,0:T(8,128)S(1)}, f32[27,256]{1,0:T(8,128)}, u32[]{:S(2)}) copy-start(f32[27,256]{1,0:T(8,128)} %refs_2_.1) | copy-start | bytes 82948
  43.2 6.0 %copy-start.4 = (bf16[256,768]{0,1:T(8,128)(2,1)S(1)}, bf16[256,768]{0,1:T(8,128)(2,1)}, u32[]{:S(2)}) copy-start(bf16[256,768]{0,1:T(8,128)(2,1)} %get-tuple-element.192) | copy-start | bytes 1179652
  43.3 7.4 %copy-start.6 = (bf16[256,256]{0,1:T(8,128)(2,1)S(1)}, bf16[256,256]{0,1:T(8,128)(2,1)}, u32[]{:S(2)}) copy-start(bf16[256,256]{0,1:T(8,128)(2,1)} %get-tuple-element.187) | copy-start | bytes 393220
  45.1 1.0 copy-start.20
  46.0 0.6 copy-start.13
  52.3 2.7 copy-start.7
  52.3 2.8 copy-start.10
  52.3 3.4 copy-start.11
  52.3 4.0 %copy-start.12 = (f32[2,19,256]{2,0,1:T(2,128)S(1)}, f32[2,19,256]{2,0,1:T(2,128)}, u32[]{:S(2)}) copy-start(f32[2,19,256]{2,0,1:T(2,128)} %param.45) | copy-start | bytes 116740
  52.3 4.6 %copy-start.9 = (bf16[9,3,256]{2,1,0:T(4,128)(2,1)S(1)}, bf16[9,3,256]{2,1,0:T(4,128)(2,1)}, u32[]{:S(2)}) copy-start(bf16[9,3,256]{2,1,0:T(4,128)(2,1)} %reshape.145) | copy-start | bytes 41476
Sparse Core Ops, SparseCore 0:
  9.6 24.5 all-gather.4
  35.8 51.2 all-gather.2
where the time goes:
time: 386 us; the launch traced here: 379 us
  Pallas kernels  305 us (79%)
  local copies, waits for them, and re-layouts  28.2 us (7%)
  other arithmetic  17.6 us (5%)
  between operations  15.6 us (4%)
  starting transfers between devices  9.15 us (2%)
    pallas_call x1, Pallas kernels, exchange(): pl.pallas_call(functools.partial(exchange_kernel, (pairs, tall, quads, sh...  131 us
    pallas_call x1, Pallas kernels, main_part(): pl.pallas_call(functools.partial(second_kernel, tall, short), grid=(n //...  131 us
    pallas_call x1, Pallas kernels, forward_part(): pl.pallas_call(first_kernel, grid=(n // chunk,), in_specs=[pl.BlockSpec(m...  25.7 us
    pallas_call x1, Pallas kernels, finish(): pl.pallas_call(finish_kernel, grid=(batch,), in_specs=[pl.BlockSpec(memor...  17.8 us
    unnamed x54, local copies, waits for them, and re-layouts  11.9 us
  transfers between devices with their start and end apart: 4, of which 0 were waited for; matrix products, arithmetic and copies ran while one was open for 11% of the time, Pallas kernels for 76%

commit v1 on v0

--- a/solution.py
+++ b/solution.py
@@ -23,7 +23,7 @@
 DECAY = 0.01
 EMA_TOP = 0.9999
 VMEM_LIMIT = 60 << 20
-CHUNK = 8
+CHUNK = 4
 FORWARD_CHUNK = 4
 GROUP = 2
 COUNT = 2048.0
@@ -641,10 +641,18 @@
 MESH = pl.DeviceIdType.MESH
 MISC_ROWS = (640, 640, 512, 80, 80, 24, 8)
 MISC_TOTAL = 2048
+SPLIT_A = 11
+SPLIT_B = 4
+LAG = 3
 
 
 def padded_rows(total, parts):
     return -(-total // (8 * parts)) * 8
+
+
+def factors(rows):
+    low = max(d for d in range(1, rows + 1) if rows % d == 0 and d * d <= rows)
+    return low, rows // low
 
 
 def exchange_kernel(
@@ -661,12 +669,18 @@
     out_b,
     shard_grad,
     norm_out,
+    own_a,
+    own_b,
     half_a,
     half_b,
-    row_a,
-    row_b,
+    near_a,
+    near_b,
+    far_a,
+    far_b,
     deep_a,
     deep_b,
+    piece_a,
+    piece_b,
     shard_weight,
     shard_first,
     shard_second,
@@ -674,10 +688,13 @@
     square_rows,
     square_deep,
     local_sem,
+    own_sem,
     core_send,
     core_recv,
-    row_send,
-    row_recv,
+    near_send,
+    near_recv,
+    far_send,
+    far_recv,
     deep_send,
     deep_recv,
     shard_send,
@@ -686,24 +703,40 @@
     square_recv,
     deep_send_two,
     deep_recv_two,
-    row_send_two,
-    row_recv_two,
+    near_send_two,
+    near_recv_two,
+    far_send_two,
+    far_recv_two,
     core_send_two,
     core_recv_two,
+    keep_sem,
 ):
-    depth, _, rows, piece, _ = grads_a.shape
-    lanes = grads_b.shape[3]
+    depth, _, tops, wide, piece, _ = grads_a.shape
+    lanes = grads_b.shape[4]
+    rows = tops * wide
     pairs, tall, quads, short = shard_shape
     batch, r = lax.axis_index("batch"), lax.axis_index("rows")
     z, c = batch // 2, batch % 2
+    y, x = r // wide, r % wide
     partner = z * 2 + (1 - c)
     row_peers = [(r + d) % rows for d in range(1, rows)]
     deep_peers = [(z + d) % depth for d in range(1, depth)]
+    x_peers = [(x + d) % wide for d in range(1, wide)]
+    y_peers = [(y + d) % tops for d in range(1, tops)]
 
     def remote(src, dst, send, recv, where):
         return pltpu.make_async_remote_copy(
             src_ref=src, dst_ref=dst, send_sem=send, recv_sem=recv, device_id=where, device_id_type=MESH
         )
+
+    def begin(copies):
+        for copy in copies:
+            copy.start()
+        return copies
+
+    def arrived(copies):
+        for copy in copies:
+            copy.wait_recv()
 
     def blocks(kernel_ref, attention_ref, flat, base, offset):
         copies = []
@@ -713,14 +746,13 @@
             far = ref.at[own] if offset is None else ref.at[own, pl.ds(offset * size, size)]
             near = flat.at[pl.ds(at, size)]
             copies.append(pltpu.make_async_copy(far, near, local_sem.at[base * (pairs + quads) + k]))
-        for copy in copies:
-            copy.start()
-        return copies
-
-    fetches = (
-        blocks(weight_kernel, weight_attention, shard_weight, 0, batch)
-        + blocks(state_kernel.at[0], state_attention.at[0], shard_first, 1, None)
-        + blocks(state_kernel.at[1], state_attention.at[1], shard_second, 2, None)
+        return begin(copies)
+
+    owns = begin(
+        [
+            pltpu.make_async_copy(grads_b.at[:, c], own_b, own_sem.at[0]),
+            pltpu.make_async_copy(grads_a.at[:, c], own_a, own_sem.at[1]),
+        ]
     )
 
     barrier = pltpu.get_barrier_semaphore()
@@ -731,232 +763,306 @@
         pl.semaphore_signal(barrier, inc=1, device_id=(peer * 2 + c, r), device_id_type=MESH)
     pl.semaphore_wait(barrier, rows + depth - 1)
 
-    cut = (piece // 8 + 1) // 2 * 8
-    chunks = [
-        (grads_b, half_b, row_b, deep_b, 0, lanes),
-        (grads_a, half_a, row_a, deep_a, 0, cut),
-        (grads_a, half_a, row_a, deep_a, cut, piece - cut),
-    ]
-    pending = []
+    set_a = (grads_a, own_a, half_a, near_a, far_a, deep_a, piece_a, out_a)
+    set_b = (grads_b, own_b, half_b, near_b, far_b, deep_b, piece_b, out_b)
+    chunks = []
+    for group, height, parts in ((set_b, lanes, SPLIT_B), (set_a, piece, SPLIT_A)):
+        marks = [height // 8 * k // parts * 8 for k in range(parts + 1)]
+        for low, high in zip(marks[:-1], marks[1:]):
+            if high > low:
+                chunks.append(group + (low, high - low, len(chunks) % 2 == 0))
+    count = len(chunks)
+    small = sum(1 for chunk in chunks if chunk[0] is grads_b)
 
     core_copies = []
-    for k, (grads, half, _, _, at, size) in enumerate(chunks):
-        copy = remote(
-            grads.at[:, 1 - c, :, pl.ds(at, size)],
-            half.at[:, :, pl.ds(at, size)],
-            core_send.at[k],
-            core_recv.at[k],
-            (partner, r),
+    for k, (grads, _, half, _, _, _, _, _, at, size, _) in enumerate(chunks):
+        span = pl.ds(at, size)
+        core_copies.append(
+            begin(
+                [
+                    remote(
+                        grads.at[:, 1 - c, :, :, span],
+                        half.at[:, :, :, span],
+                        core_send.at[k],
+                        core_recv.at[k],
+                        (partner, r),
+                    )
+                ]
+            )
         )
-        copy.start()
-        core_copies.append(copy)
-    row_copies = []
-    for k, (grads, half, row, _, at, size) in enumerate(chunks):
-        core_copies[k].wait_recv()
-
-        def add_own(t, carry, grads=grads, half=half, at=at, size=size):
-            i, j = t // rows, t % rows
-            span = pl.ds(at, size)
-            half[i, j, span] = half[i, j, span] + grads[i, c, j, span]
+    fetches = (
+        blocks(weight_kernel, weight_attention, shard_weight, 0, batch)
+        + blocks(state_kernel.at[0], state_attention.at[0], shard_first, 1, None)
+        + blocks(state_kernel.at[1], state_attention.at[1], shard_second, 2, None)
+    )
+    near_copies, far_copies, deep_copies = [], [], []
+
+    def sum_near(k):
+        _, own, half, near, _, _, _, _, at, size, x_first = chunks[k]
+        if k == 0:
+            owns[0].wait()
+        if k == small:
+            owns[1].wait()
+        arrived(core_copies[k])
+        span = pl.ds(at, size)
+
+        def add_own(t, carry):
+            i, j, l = t // rows, t // wide % tops, t % wide
+            half[i, j, l, span] = half[i, j, l, span] + own[i, j, l, span]
             return carry
 
         lax.fori_loop(0, depth * rows, add_own, 0)
         copies = []
-        for d, peer in enumerate(row_peers):
-            copy = remote(
-                half.at[:, peer, pl.ds(at, size)],
-                row.at[d, :, pl.ds(at, size)],
-                row_send.at[k, d],
-                row_recv.at[k, d],
-                (batch, peer),
+        for d, peer in enumerate(x_peers if x_first else y_peers):
+            src = half.at[:, :, peer, span] if x_first else half.at[:, peer, :, span]
+            dst = near.at[d, :, pl.ds(0, tops if x_first else wide), span]
+            where = (batch, y * wide + peer) if x_first else (batch, peer * wide + x)
+            copies.append(remote(src, dst, near_send.at[k, d], near_recv.at[k, d], where))
+        near_copies.append(begin(copies))
+
+    def sum_far(k):
+        _, _, half, near, far, _, _, _, at, size, x_first = chunks[k]
+        arrived(near_copies[k])
+        span = pl.ds(at, size)
+        across = tops if x_first else wide
+
+        def add_near(t, carry):
+            i, j = t // across, t % across
+            place = (i, j, x) if x_first else (i, y, j)
+            total = half[place + (span,)]
+            for d in range((wide if x_first else tops) - 1):
+                total = total + near[d, i, j, span]
+            half[place + (span,)] = total
+            return carry
+
+        lax.fori_loop(0, depth * across, add_near, 0)
+        copies = []
+        for d, peer in enumerate(y_peers if x_first else x_peers):
+            src = half.at[:, peer, x, span] if x_first else half.at[:, y, peer, span]
+            where = (batch, peer * wide + x) if x_first else (batch, y * wide + peer)
+            copies.append(
+                remote(src, far.at[d, :, span], far_send.at[k, d], far_recv.at[k, d], where)
             )
-            copy.start()
-            copies.append(copy)
-        row_copies.append(copies)
-    deep_copies = []
-    for k, (grads, half, row, deep, at, size) in enumerate(chunks):
-        for copy in row_copies[k]:
-            copy.wait_recv()
-
-        def add_rows(i, carry, half=half, row=row, at=at, size=size):
-            span = pl.ds(at, size)
-            total = half[i, r, span]
-            for d in range(rows - 1):
-                total = total + row[d, i, span]
-            half[i, r, span] = total
+        far_copies.append(begin(copies))
+
+    def sum_deep(k):
+        _, _, half, _, far, deep, _, _, at, size, x_first = chunks[k]
+        arrived(far_copies[k])
+        span = pl.ds(at, size)
+
+        def add_far(i, carry):
+            total = half[i, y, x, span]
+            for d in range((tops if x_first else wide) - 1):
+                total = total + far[d, i, span]
+            half[i, y, x, span] = total
             return carry
 
-        lax.fori_loop(0, depth, add_rows, 0)
+        lax.fori_loop(0, depth, add_far, 0)
         copies = []
         for d, peer in enumerate(deep_peers):
-            copy = remote(
-                half.at[peer, r, pl.ds(at, size)],
-                deep.at[d, pl.ds(at, size)],
-                deep_send.at[k, d],
-                deep_recv.at[k, d],
-                (peer * 2 + c, r),
+            copies.append(
+                remote(
+                    half.at[peer, y, x, span],
+                    deep.at[d, span],
+                    deep_send.at[k, d],
+                    deep_recv.at[k, d],
+                    (peer * 2 + c, r),
+                )
             )
-            copy.start()
-            copies.append(copy)
-        deep_copies.append(copies)
-
-    def finish(k):
-        _, half, _, deep, at, size = chunks[k]
-        for copy in deep_copies[k]:
-            copy.wait_recv()
+        deep_copies.append(begin(copies))
+
+    def finish_sum(k):
+        _, _, half, _, _, deep, _, _, at, size, _ = chunks[k]
+        arrived(deep_copies[k])
         span = pl.ds(at, size)
-        total = half[z, r, span]
+        total = half[z, y, x, span]
         for d in range(depth - 1):
             total = total + deep[d, span]
         return total
 
-    def squares(x):
-        return jnp.sum((x * x).reshape(-1, 8, 256), axis=0)
-
-    def gather(bufs, k, at, size, stage):
+    def squares(values):
+        return jnp.sum((values * values).reshape(-1, 8, 256), axis=0)
+
+    def gather_deep(k):
+        _, _, _, _, _, _, part, out, at, size, _ = chunks[k]
         span = pl.ds(at, size)
+        keep = pltpu.make_async_copy(part.at[span], out.at[z, c, y, x, span], keep_sem.at[k])
+        keep.start()
         copies = []
-        if stage == 0:
-            for d, peer in enumerate(deep_peers):
-                copies.append(
-                    remote(
-                        bufs.at[z, c, r, span],
-                        bufs.at[z, c, r, span],
-                        deep_send_two.at[k, d],
-                        deep_recv_two.at[k, d],
-                        (peer * 2 + c, r),
-                    )
-                )
-        elif stage == 1:
-            for d, peer in enumerate(row_peers):
-                copies.append(
-                    remote(
-                        bufs.at[:, c, r, span],
-                        bufs.at[:, c, r, span],
-                        row_send_two.at[k, d],
-                        row_recv_two.at[k, d],
-                        (batch, peer),
-                    )
-                )
-        else:
+        for d, peer in enumerate(deep_peers):
             copies.append(
                 remote(
-                    bufs.at[:, c, :, span],
-                    bufs.at[:, c, :, span],
-                    core_send_two.at[k],
-                    core_recv_two.at[k],
-                    (partner, r),
+                    part.at[span],
+                    out.at[z, c, y, x, span],
+                    deep_send_two.at[k, d],
+                    deep_recv_two.at[k, d],
+                    (peer * 2 + c, r),
                 )
             )
-        for copy in copies:
-            copy.start()
-        return copies
-
-    total = finish(0)
-    out_b[z, c, r] = total
-    stage_zero = [gather(out_b, 0, 0, lanes, 0)]
-    line = (batch * rows + r) * lanes + lax.broadcasted_iota(jnp.int32, total.shape, 0)
-    square = squares(jnp.where(line < sum(MISC_ROWS[:-1]), total, 0.0))
-    for k in (1, 2):
-        total = finish(k)
-        shard_grad[r, pl.ds(chunks[k][4], chunks[k][5])] = total
-        square = square + squares(total)
+        return keep, begin(copies)
+
+    def gather_near(k):
+        _, _, _, _, _, _, _, out, at, size, x_first = chunks[k]
+        place = out.at[:, c, y, x, pl.ds(at, size)]
+        copies = []
+        for d, peer in enumerate(y_peers if x_first else x_peers):
+            where = (batch, peer * wide + x) if x_first else (batch, y * wide + peer)
+            copies.append(remote(place, place, near_send_two.at[k, d], near_recv_two.at[k, d], where))
+        return begin(copies)
+
+    def gather_far(k):
+        _, _, _, _, _, _, _, out, at, size, x_first = chunks[k]
+        span = pl.ds(at, size)
+        place = out.at[:, c, :, x, span] if x_first else out.at[:, c, y, :, span]
+        copies = []
+        for d, peer in enumerate(x_peers if x_first else y_peers):
+            where = (batch, y * wide + peer) if x_first else (batch, peer * wide + x)
+            copies.append(remote(place, place, far_send_two.at[k, d], far_recv_two.at[k, d], where))
+        return begin(copies)
+
+    def gather_core(k):
+        _, _, _, _, _, _, _, out, at, size, _ = chunks[k]
+        place = out.at[:, c, :, :, pl.ds(at, size)]
+        return begin([remote(place, place, core_send_two.at[k], core_recv_two.at[k], (partner, r))])
+
+    keeps, firsts, seconds, thirds, lasts = [], [], [], [], []
+    partial = []
+
+    def send_deep(k):
+        keep, copies = gather_deep(k)
+        keeps.append(keep)
+        firsts.append(copies)
+
+    def send_near(k):
+        keeps[k].wait()
+        arrived(firsts[k])
+        seconds.append(gather_near(k))
+
+    def send_far(k):
+        arrived(seconds[k])
+        thirds.append(gather_far(k))
+
+    def send_core(k):
+        arrived(thirds[k])
+        lasts.append(gather_core(k))
+
+    def sum_last(k):
+        total = finish_sum(k)
+        at, size = chunks[k][8], chunks[k][9]
+        counted = total
+        if k < small:
+            piece_b[pl.ds(at, size)] = total
+            line = (batch * rows + r) * lanes + at + lax.broadcasted_iota(jnp.int32, total.shape, 0)
+            counted = jnp.where(line < sum(MISC_ROWS[:-1]), total, 0.0)
+            send_deep(k)
+        else:
+            shard_grad[r, pl.ds(at, size)] = total
+        partial.append(squares(counted))
+
+    for t in range(count + 3 * LAG):
+        for stage, lag in ((sum_near, 0), (sum_far, LAG), (sum_deep, 2 * LAG), (sum_last, 3 * LAG)):
+            if 0 <= t - lag < count:
+                stage(t - lag)
+    square = sum(partial)
     square_core[0] = square
-    copy = remote(square_core.at[0], square_core.at[1], square_send.at[0], square_recv.at[0], (partner, r))
-    copy.start()
-    pending.append(copy)
-    shard_copies = []
-    for d, peer in enumerate(row_peers):
-        share = remote(
-            shard_grad.at[r], shard_grad.at[r], shard_send.at[d], shard_recv.at[d], (batch, peer)
-        )
-        share.start()
-        shard_copies.append(share)
-    copy.wait_recv()
+    square_copies = begin(
+        [remote(square_core.at[0], square_core.at[1], square_send.at[0], square_recv.at[0], (partner, r))]
+    )
+    shard_copies = begin(
+        [
+            remote(shard_grad.at[r], shard_grad.at[r], shard_send.at[d], shard_recv.at[d], (batch, peer))
+            for d, peer in enumerate(row_peers)
+        ]
+    )
+    arrived(square_copies)
     square_rows[r] = square_core[0] + square_core[1]
-    copies = []
-    for d, peer in enumerate(row_peers):
-        copy = remote(
-            square_rows.at[r], square_rows.at[r], square_send.at[1 + d], square_recv.at[1 + d], (batch, peer)
-        )
-        copy.start()
-        copies.append(copy)
-    pending += copies
-    for copy in copies:
-        copy.wait_recv()
+    copies = begin(
+        [
+            remote(
+                square_rows.at[r],
+                square_rows.at[r],
+                square_send.at[1 + d],
+                square_recv.at[1 + d],
+                (batch, peer),
+            )
+            for d, peer in enumerate(row_peers)
+        ]
+    )
+    for k in range(small):
+        send_near(k)
+    arrived(copies)
+    square_copies += copies
     square_deep[z] = sum(square_rows[j] for j in range(rows))
-    copies = []
-    for d, peer in enumerate(deep_peers):
-        copy = remote(
-            square_deep.at[z],
-            square_deep.at[z],
-            square_send.at[rows + d],
-            square_recv.at[rows + d],
-            (peer * 2 + c, r),
-        )
-        copy.start()
-        copies.append(copy)
-    pending += copies
-    for copy in copies:
-        copy.wait_recv()
+    copies = begin(
+        [
+            remote(
+                square_deep.at[z],
+                square_deep.at[z],
+                square_send.at[rows + d],
+                square_recv.at[rows + d],
+                (peer * 2 + c, r),
+            )
+            for d, peer in enumerate(deep_peers)
+        ]
+    )
+    for fetch in fetches:
+        fetch.wait()
+    for k in range(small):
+        send_far(k)
+    arrived(copies)
+    square_copies += copies
     square = sum(square_deep[j] for j in range(depth))
     norm = jnp.sqrt(jnp.sum(jnp.sum(square, axis=0, keepdims=True), axis=1, keepdims=True))
     clip = CLIP / jnp.maximum(norm, CLIP)
     norm_out[...] = jnp.broadcast_to(norm, norm_out.shape)
-
-    def moments(at, g):
-        span = pl.ds(at, piece)
+    for k in range(small, count):
+        at, size = chunks[k][8], chunks[k][9]
+        span = pl.ds(pl.multiple_of(r * piece + at, 8), size)
+        g = shard_grad[r, pl.ds(at, size)] * clip
         first = BETA_ONE * shard_first[span] + (1.0 - BETA_ONE) * g
         second = BETA_TWO * shard_second[span] + (1.0 - BETA_TWO) * g * g
-        return first, second
-
-    for fetch in fetches:
-        fetch.wait()
-    mine = pl.multiple_of(r * piece, 8)
-    first, second = moments(mine, shard_grad[r] * clip)
-    line = mine + lax.broadcasted_iota(jnp.int32, first.shape, 0)
-    rate = jnp.where(line < pairs * tall, rates[0], rates[1])
-    weight = shard_weight[pl.ds(mine, piece)]
-    step = first * scalars[0] / (jnp.sqrt(second * scalars[1]) + EPS_ADAM)
-    out_a[z, c, r] = weight - rate * (step + DECAY * weight)
-    for k in (1, 2):
-        stage_zero.append(gather(out_a, k, chunks[k][4], chunks[k][5], 0))
-    stage_one, stage_two = [], []
-    for k in range(3):
-        for copy in stage_zero[k]:
-            copy.wait_recv()
-        stage_one.append(gather(out_b if k == 0 else out_a, k, chunks[k][4], chunks[k][5], 1))
-    for k in range(3):
-        for copy in stage_one[k]:
-            copy.wait_recv()
-        stage_two.append(gather(out_b if k == 0 else out_a, k, chunks[k][4], chunks[k][5], 2))
-    for copy in shard_copies:
-        copy.wait_recv()
-    for copies in stage_two:
+        line = r * piece + at + lax.broadcasted_iota(jnp.int32, g.shape, 0)
+        rate = jnp.where(line < pairs * tall, rates[0], rates[1])
+        weight = shard_weight[span]
+        step = first * scalars[0] / (jnp.sqrt(second * scalars[1]) + EPS_ADAM)
+        piece_a[pl.ds(at, size)] = weight - rate * (step + DECAY * weight)
+        send_deep(k)
+    for k in range(small):
+        send_core(k)
+    for t in range(small, count + 2 * LAG):
+        for stage, lag in ((send_near, 0), (send_far, LAG), (send_core, 2 * LAG)):
+            if small <= t - lag < count:
+                stage(t - lag)
+    arrived(shard_copies)
+    for copies in lasts:
+        arrived(copies)
+    for copies in (
+        core_copies + near_copies + far_copies + deep_copies + firsts + seconds + thirds + lasts
+    ):
         for copy in copies:
-            copy.wait_recv()
-    pending += core_copies + shard_copies
-    for copies in row_copies + deep_copies + stage_zero + stage_one + stage_two:
-        pending += copies
-    for copy in pending:
+            copy.wait_send()
+    for copy in square_copies + shard_copies:
         copy.wait_send()
 
 
 def exchange(grads_a, grads_b, state_kernel, state_attention, weight_kernel, weight_attention, scalars):
     depth, _, rows, piece, width = grads_a.shape
+    tops, wide = factors(rows)
     lanes = grads_b.shape[3]
+    grads_a = grads_a.reshape(depth, 2, tops, wide, piece, width)
+    grads_b = grads_b.reshape(depth, 2, tops, wide, lanes, width)
     pairs, tall = state_kernel.shape[1:3]
     quads, short = state_attention.shape[1:3]
     shape = functools.partial(jax.ShapeDtypeStruct, dtype=jnp.float32)
     whole = pl.BlockSpec(memory_space=pltpu.VMEM)
+    anywhere = pl.BlockSpec(memory_space=pl.ANY)
     dma = pltpu.SemaphoreType.DMA
     vmem = functools.partial(pltpu.VMEM, dtype=jnp.float32)
+    most = max(tops, wide)
     return pl.pallas_call(
         functools.partial(exchange_kernel, (pairs, tall, quads, short), (RATES[1], RATES[2])),
-        in_specs=[whole] * 2
-        + [pl.BlockSpec(memory_space=pl.ANY)] * 4
-        + [pl.BlockSpec(memory_space=pltpu.SMEM)],
-        out_specs=[whole] * 4,
+        in_specs=[anywhere] * 6 + [pl.BlockSpec(memory_space=pltpu.SMEM)],
+        out_specs=[anywhere] * 2 + [whole] * 2,
         out_shape=[
             shape(grads_a.shape),
             shape(grads_b.shape),
@@ -964,12 +1070,18 @@
             shape((8, 128)),
         ],
         scratch_shapes=[
-            vmem((depth, rows, piece, width)),
-            vmem((depth, rows, lanes, width)),
-            vmem((rows - 1, depth, piece, width)),
-            vmem((rows - 1, depth, lanes, width)),
+            vmem((depth, tops, wide, piece, width)),
+            vmem((depth, tops, wide, lanes, width)),
+            vmem((depth, tops, wide, piece, width)),
+            vmem((depth, tops, wide, lanes, width)),
+            vmem((most - 1, depth, most, piece, width)),
+            vmem((most - 1, depth, most, lanes, width)),
+            vmem((most - 1, depth, piece, width)),
+            vmem((most - 1, depth, lanes, width)),
             vmem((depth - 1, piece, width)),
             vmem((depth - 1, lanes, width)),
+            vmem((piece, width)),
+            vmem((lanes, width)),
             vmem((rows * piece, width)),
             vmem((rows * piece, width)),
             vmem((rows * piece, width)),
@@ -977,22 +1089,28 @@
             vmem((rows, 8, width)),
             vmem((depth, 8, width)),
             dma((3 * (pairs + quads),)),
-            dma((3,)),
-            dma((3,)),
-            dma((3, rows - 1)),
-            dma((3, rows - 1)),
-            dma((3, depth - 1)),
-            dma((3, depth - 1)),
+            dma((2,)),
+            dma((SPLIT_A + SPLIT_B,)),
+            dma((SPLIT_A + SPLIT_B,)),
+            dma((SPLIT_A + SPLIT_B, most - 1)),
+            dma((SPLIT_A + SPLIT_B, most - 1)),
+            dma((SPLIT_A + SPLIT_B, most - 1)),
+            dma((SPLIT_A + SPLIT_B, most - 1)),
+            dma((SPLIT_A + SPLIT_B, depth - 1)),
+            dma((SPLIT_A + SPLIT_B, depth - 1)),
             dma((rows - 1,)),
             dma((rows - 1,)),
             dma((rows + depth - 1,)),
             dma((rows + depth - 1,)),
-            dma((3, depth - 1)),
-            dma((3, depth - 1)),
-            dma((3, rows - 1)),
-            dma((3, rows - 1)),
-            dma((3,)),
-            dma((3,)),
+            dma((SPLIT_A + SPLIT_B, depth - 1)),
+            dma((SPLIT_A + SPLIT_B, depth - 1)),
+            dma((SPLIT_A + SPLIT_B, most - 1)),
+            dma((SPLIT_A + SPLIT_B, most - 1)),
+            dma((SPLIT_A + SPLIT_B, most - 1)),
+            dma((SPLIT_A + SPLIT_B, most - 1)),
+            dma((SPLIT_A + SPLIT_B,)),
+            dma((SPLIT_A + SPLIT_B,)),
+            dma((SPLIT_A + SPLIT_B,)),
         ],
         compiler_params=pltpu.CompilerParams(
             collective_id=0, has_side_effects=True, vmem_limit_bytes=VMEM_LIMIT

time: 386 us -> 339 us (0.88); the launches traced: 379 us -> 338 us
  Pallas kernels: 305 us -> 265 us
    pallas_call x1, Pallas kernels: 131 us -> 102 us  [exchange(): pl.pallas_call(functools.partial(exchange_kernel, (pairs, tall, quads, sh...]
    pallas_call x1, Pallas kernels: 131 us -> 119 us  [main_part(): pl.pallas_call(functools.partial(second_kernel, tall, short), grid=(n //...]
  transfers between devices with their start and end apart: 4 -> 4, of which waited for: 0 -> 0; matrix products, arithmetic and copies ran while one was open for 11% -> 12% of each run, Pallas kernels for 76% -> 73%
where the time goes in v1:
time: 339 us; the launch traced here: 338 us
  Pallas kernels  265 us (78%)
  local copies, waits for them, and re-layouts  28.2 us (8%)
  other arithmetic  17.6 us (5%)
  between operations  15.3 us (5%)
  starting transfers between devices  9.15 us (3%)
    pallas_call x1, Pallas kernels, main_part(): pl.pallas_call(functools.partial(second_kernel, tall, short), grid=(n //...  119 us
    pallas_call x1, Pallas kernels, exchange(): pl.pallas_call(functools.partial(exchange_kernel, (pairs, tall, quads, sh...  102 us
    pallas_call x1, Pallas kernels, forward_part(): pl.pallas_call(first_kernel, grid=(n // chunk,), in_specs=[pl.BlockSpec(m...  25.8 us
    pallas_call x1, Pallas kernels, finish(): pl.pallas_call(finish_kernel, grid=(batch,), in_specs=[pl.BlockSpec(memor...  17.8 us
    unnamed x54, local copies, waits for them, and re-layouts  11.9 us
    convert_element_type x1, other arithmetic, local(): keep = keep_mask.reshape(rows, own, -1, chans).astype(jnp.bfloat16)  6.84 us
  transfers between devices with their start and end apart: 4, of which 0 were waited for; matrix products, arithmetic and copies ran while one was open for 12% of the time, Pallas kernels for 73%

profile of v1, /device:TPU:1, one launch (start us, length us, event | category | flops | bytes accessed | tf_op | source)
XLA Modules:
  0.0 338.3 jit_solution(15438114682476834136)
XLA Ops:
  7.9 1.0 pad_maximum_fusion.1
  9.7 1.0 reshape.148
  10.7 4.3 %all-to-all-start = ((f32[4,1,16384]{2,1,0:T(1,128)}), f32[4,1,16384]{2,1,0:T(1,128)}, u32[]{:S(2)}, u32[]{:S(2)}) async-start(f32[4,1,16384]{2,1,0:T(1,128)} %reshape.148), calls=%async_computation | async-start | bytes 524288 | tf_op jit(solution)/shard_map/all_to_all | solution.py:1303
  15.0 0.7 all-gather.3.cloned.1.call-update
  15.7 6.8 %convert_element_type.51 = bf16[128,4,16,256]{3,2,1,0:T(8,128)(2,1)} convert(s32[128,4,16,256]{3,2,1,0:T(8,128)} %param.30) | non-fusion elementwise | flops 2097152 | bytes 12582912 | tf_op jit(solution)/shard_map/convert_element_type | solution.py:1304
  22.6 0.8 slice_bitcast_fusion.5
  23.4 1.4 fusion.9
  26.0 0.9 convert_element_type.56
  27.5 0.7 convert_element_type.59.shift_low
  28.3 2.7 convert_element_type.61
  31.0 1.0 copy.79
  32.0 1.8 slice_bitcast_fusion.3
  35.1 4.8 %all-to-all-start.1 = ((bf16[4,32,64,256]{3,2,1,0:T(8,128)(2,1)}), bf16[4,32,64,256]{3,2,1,0:T(8,128)(2,1)}, u32[]{:S(2)}, u32[]{:S(2)}) async-start(bf16[4,32,64,256]{3,2,1,0:T(8,128)(2,1)} %bitcast.64), calls=%async_computation.1 | async-start | bytes 8388608 | tf_op jit(solution)/shard_map/all_to_all | solution.py:1330
  40.6 0.9 fusion.6
  41.5 1.7 fusion.8
  43.4 0.9 copy-done.2
  44.3 0.8 add_multiply_fusion.1
  45.1 0.9 add_multiply_fusion
  47.2 0.8 slice.61.time_two
  49.3 0.9 copy.81.qkv
  50.8 0.8 copy.82.proj
  52.3 1.1 rev.7
  53.4 1.5 copy.77
  58.7 2.3 reduce
  61.0 1.1 reshape.149.pair
  62.1 25.8 %forward_part.1 = (f32[32,256,256]{2,1,0:T(8,128)}, f32[32,256,256]{2,1,0:T(8,128)}, f32[32,8,256]{2,1,0:T(8,128)}, f32[32,8,256]{2,1,0:T(8,128)}, f32[32,8,256]{2,1,0:T(8,128)}) custom-call(f32[2,32]{1,0:T(2,128)} %pad_maximum_fusion.4.mix, f32[4,32,8,64]{3,2,1,0:T(8,128)} %reshape.149.pair, f32[32,1,256]{2,1,0:T(1,128)} %broadcast_in_dim.6.tshift, ...), custom_call_target="tpu_custom_call" | custom-call | flops 10066329600 | bytes 16777216 | tf_op jit(solution)/shard_map/forward_part/pallas_call | solution.py:576
  87.8 119.1 %main_part.1 = (f32[8,704,256]{2,1,0:T(8,128)}, f32[2048,256]{1,0:T(8,128)}) custom-call(f32[32]{0:T(128)} %get-tuple-element.206.coef, f32[32,256,256]{2,1,0:T(8,128)} %get-tuple-element.74.start_in, f32[32,256,256]{2,1,0:T(8,128)} %get-tuple-element.75.inner_in, f32[32,8,256]{2,1,0:T(8,128)} %get-tuple-element.76.stats_in, ...), custom_call_target="tpu_custom_call" | custom-call | flops 75161927680 | bytes 20971520 | tf_op jit(solution)/shard_map/main_part/pallas_call | solution.py:603
  207.0 102.1 %exchange.1 = (f32[4,2,2,2,176,256]{5,4,3,2,1,0:T(8,128)}, f32[4,2,2,2,64,256]{5,4,3,2,1,0:T(8,128)}, f32[4,176,256]{2,1,0:T(8,128)}, f32[8,128]{1,0:T(8,128)}) custom-call(f32[4,2,2,2,176,256]{5,4,3,2,1,0:T(8,128)} %bitcast.65, f32[4,2,2,2,64,256]{5,4,3,2,1,0:T(8,128)} %bitcast.69, f32[2,2,288,256]{3,2,1,0:T(8,128)} %state_kernel.3, ...), custom_call_target="tpu_custom_call" | custom-call | tf_op jit(solution)/shard_map/exchange/pallas_call | solution.py:1062
  309.2 17.8 %finish.1 = (f32[2,2,2304,256]{3,2,1,0:T(8,128)}, f32[2,4,256,256]{3,2,1,0:T(8,128)}, f32[2,640,512]{2,1,0:T(8,128)}, f32[2,512,256]{2,1,0:T(8,128)}, f32[2,27,2...) custom-call(f32[3]{0:T(128)} %pad_maximum_fusion.5.scalars, ...), custom_call_target="tpu_custom_call" | custom-call | flops 41943040 | bytes 37748736 | tf_op jit(solution)/shard_map/finish/pallas_call | solution.py:1209
  327.0 1.5 copy.86
  328.5 1.5 copy.87
  330.0 1.4 copy.88
  (79 shorter events, 11.9 us)
Async XLA Ops:
  7.2 301.9 %all-gather.5.cloned.1.call-start = ((), (), s32[]{:S(2)}) async-start(), calls=%async_computation.3 | async-start | bytes 1179648 | tf_op jit(solution)/shard_map/all_gather | solution.py:1418
  10.7 24.4 %all-to-all-start = ((f32[4,1,16384]{2,1,0:T(1,128)}), f32[4,1,16384]{2,1,0:T(1,128)}, u32[]{:S(2)}, u32[]{:S(2)}) async-start(f32[4,1,16384]{2,1,0:T(1,128)} %reshape.148), calls=%async_computation | async-start | bytes 524288 | tf_op jit(solution)/shard_map/all_to_all | solution.py:1303
  15.0 294.2 %all-gather.3.cloned.1.call-start = ((), (), s32[]{:S(2)}) async-start(), calls=%async_computation.2 | async-start | bytes 5308416 | tf_op jit(solution)/shard_map/all_gather | solution.py:1417
  15.7 10.3 %copy-start = (f32[640,512]{1,0:T(8,128)S(1)}, f32[640,512]{1,0:T(8,128)}, u32[]{:S(2)}) copy-start(f32[640,512]{1,0:T(8,128)} %refs_0_.1) | copy-start | bytes 3932164
  22.6 5.0 %copy-start.3 = (f32[512,256]{1,0:T(8,128)S(1)}, f32[512,256]{1,0:T(8,128)}, u32[]{:S(2)}) copy-start(f32[512,256]{1,0:T(8,128)} %refs_1_.1) | copy-start | bytes 1572868
  28.3 2.7 copy-start.1
  31.0 3.0 copy-start.19
  31.0 3.3 copy-start.16
  34.3 9.0 %copy-start.14 = (bf16[32,128]{1,0:T(8,128)(2,1)}, bf16[32,128]{1,0:T(8,128)(2,1)S(1)}, u32[]{:S(2)}) copy-start(bf16[32,128]{1,0:T(8,128)(2,1)S(1)} %pad_maximum_fusion.2.embed) | copy-start | bytes 24580
  35.1 52.7 %all-to-all-start.1 = ((bf16[4,32,64,256]{3,2,1,0:T(8,128)(2,1)}), bf16[4,32,64,256]{3,2,1,0:T(8,128)(2,1)}, u32[]{:S(2)}, u32[]{:S(2)}) async-start(bf16[4,32,64,256]{3,2,1,0:T(8,128)(2,1)} %bitcast.64), calls=%async_computation.1 | async-start | bytes 8388608 | tf_op jit(solution)/shard_map/all_to_all | solution.py:1330
  43.2 1.1 copy-start.2
  43.2 1.1 copy-start.17
  43.2 1.9 copy-start.18
  43.2 2.8 copy-start.5
  43.2 2.8 copy-start.15
  43.2 5.4 %copy-start.8 = (f32[27,256]{1,0:T(8,128)S(1)}, f32[27,256]{1,0:T(8,128)}, u32[]{:S(2)}) copy-start(f32[27,256]{1,0:T(8,128)} %refs_2_.1) | copy-start | bytes 82948
  43.2 6.0 %copy-start.4 = (bf16[256,768]{0,1:T(8,128)(2,1)S(1)}, bf16[256,768]{0,1:T(8,128)(2,1)}, u32[]{:S(2)}) copy-start(bf16[256,768]{0,1:T(8,128)(2,1)} %get-tuple-element.192) | copy-start | bytes 1179652
  43.3 7.4 %copy-start.6 = (bf16[256,256]{0,1:T(8,128)(2,1)S(1)}, bf16[256,256]{0,1:T(8,128)(2,1)}, u32[]{:S(2)}) copy-start(bf16[256,256]{0,1:T(8,128)(2,1)} %get-tuple-element.187) | copy-start | bytes 393220
  45.1 1.0 copy-start.20
  46.0 0.6 copy-start.13
  52.3 2.7 copy-start.7
  52.3 2.8 copy-start.10
  52.3 3.4 %copy-start.11 = (f32[2,27,256]{2,0,1:T(2,128)S(1)}, f32[2,27,256]{2,0,1:T(2,128)}, u32[]{:S(2)}) copy-start(f32[2,27,256]{2,0,1:T(2,128)} %param.39) | copy-start | bytes 165892
  52.3 4.0 %copy-start.12 = (f32[2,19,256]{2,0,1:T(2,128)S(1)}, f32[2,19,256]{2,0,1:T(2,128)}, u32[]{:S(2)}) copy-start(f32[2,19,256]{2,0,1:T(2,128)} %param.45) | copy-start | bytes 116740
  52.3 4.6 %copy-start.9 = (bf16[9,3,256]{2,1,0:T(4,128)(2,1)S(1)}, bf16[9,3,256]{2,1,0:T(4,128)(2,1)}, u32[]{:S(2)}) copy-start(bf16[9,3,256]{2,1,0:T(4,128)(2,1)} %reshape.139) | copy-start | bytes 41476
Sparse Core Ops, SparseCore 0:
  9.6 24.5 all-gather.4
  35.8 51.2 all-gather.2

commit v2 on v1

--- a/solution.py
+++ b/solution.py
@@ -24,7 +24,7 @@
 EMA_TOP = 0.9999
 VMEM_LIMIT = 60 << 20
 CHUNK = 4
-FORWARD_CHUNK = 4
+FORWARD_CHUNK = 8
 GROUP = 2
 COUNT = 2048.0
 RATES = (0.1, 0.01, 0.03, 0.05, 0.02, 0.01, 0.2)
@@ -155,7 +155,25 @@
 
 
 def first_kernel(
-    mix, pair, tshift, inlet, kernel_one, small, start_out, inner_out, stats_out, noisy_out, target_out, buf
+    mix,
+    pair,
+    embed,
+    time_weight,
+    shift_weight,
+    inlet,
+    kernel_one,
+    small,
+    start_out,
+    inner_out,
+    stats_out,
+    noisy_out,
+    target_out,
+    hidden_out,
+    hidden_slope_out,
+    time_act_out,
+    time_slope_out,
+    buf,
+    tshift,
 ):
     chunk = start_out.shape[0]
     step = pl.program_id(0)
@@ -163,10 +181,27 @@
     @pl.when(step == 0)
     def _():
         zero_edges(buf)
+        width = embed.shape[1]
+
+        def layer(x, weight, at):
+            bias = jnp.concatenate([small[at : at + 1], small[at + 1 : at + 2]], axis=1)
+            z = dot(x, weight.astype(jnp.bfloat16)) + bias
+            s = logistic(z)
+            return (z * s).astype(jnp.bfloat16), s * (1.0 + z * (1.0 - s))
+
+        hidden, hidden_slope = layer(embed[...], time_weight[0:width, :], 15)
+        time_act, time_slope = layer(hidden, time_weight[width:, :], 17)
+        hidden_out[...] = hidden
+        hidden_slope_out[...] = hidden_slope
+        time_act_out[...] = time_act
+        time_slope_out[...] = time_slope
+        both = small[14:15] + small[9:10]
+        tshift[...] = dot(time_act, shift_weight[...].astype(jnp.bfloat16)) + both
 
     masks = tap_masks()
     not_first, not_last = edge_masks()
-    real = lax.broadcasted_iota(jnp.int32, (8, 256), 0) < 3
+    part = pair.shape[3] // 2
+    blank = jnp.zeros((4, 256), jnp.float32)
 
     def work(images):
         n = len(images)
@@ -174,9 +209,9 @@
         low, high = images[0], images[-1] + 1
         starts = []
         for c in images:
-            both = lanes_joined([pair[s, c] for s in range(pair.shape[0])])
-            clean = jnp.where(real, both, 0.0)
-            noise = jnp.where(real, pltpu.roll(both, 5, 0), 0.0)
+            tiles = [pair[s, c] for s in range(pair.shape[0])]
+            clean = jnp.concatenate([lanes_joined([t[:, :part] for t in tiles]), blank], axis=0)
+            noise = jnp.concatenate([lanes_joined([t[:, part:] for t in tiles]), blank], axis=0)
             noisy = mix[0, step * chunk + c] * clean + mix[1, step * chunk + c] * noise
             noisy = noisy.astype(jnp.bfloat16).astype(jnp.float32)
             noisy_out[c] = noisy
@@ -195,7 +230,7 @@
         yield
         inners = []
         for i, c in enumerate(images):
-            inner = inner_all[256 * i : 256 * i + 256] + tshift[c]
+            inner = inner_all[256 * i : 256 * i + 256] + tshift[pl.ds(step * chunk + c, 1), :]
             inner_out[c] = inner
             inners.append(inner)
         mean_two, rstd_two = stats_of(inners)
@@ -250,8 +285,8 @@
     hidden_slope,
     time_act,
     time_slope,
-    time_two,
-    shift_low,
+    time_weight,
+    shift_weight,
     shard_out,
     rest_out,
     grad_one_out,
@@ -501,9 +536,10 @@
             )
         total = tshift_grad[...]
         shift_grad = full_dot(time_act[...], total, TN)
-        grad_act = full_dot(total, shift_low[...], NT) * time_slope[...]
+        grad_act = full_dot(total, shift_weight[...].astype(jnp.bfloat16), NT) * time_slope[...]
         two_grad = full_dot(hidden[...], grad_act, TN)
-        grad_hidden = full_dot(grad_act, time_two[...], NT) * hidden_slope[...]
+        time_two = time_weight[embed.shape[1] :, :].astype(jnp.bfloat16)
+        grad_hidden = full_dot(grad_act, time_two, NT) * hidden_slope[...]
         one_grad = full_dot(embed[...], grad_hidden, TN)
         width = one_grad.shape[0]
         height = width + two_grad.shape[0]
@@ -570,29 +606,37 @@
     return pl.BlockSpec((block[0], chunk) + block[2:], lambda i: (0, i, 0, 0))
 
 
-def forward_part(chunk, mix, pair, tshift, inlet, kernel_one, small):
-    n = pair.shape[1]
+def forward_part(chunk, mix, pair, embed, time_weight, shift_weight, inlet, kernel_one, small):
+    n, deep = pair.shape[1], time_weight.shape[1]
+    chunk = min(chunk, n)
     shapes = [(n, 256, 256), (n, 256, 256), (n, 8, 256), (n, 8, 256), (n, 8, 256)]
+    whole = [jnp.bfloat16, jnp.float32, jnp.bfloat16, jnp.float32]
     return pl.pallas_call(
         first_kernel,
         grid=(n // chunk,),
         in_specs=[
             pl.BlockSpec(memory_space=pltpu.SMEM),
             by_source(chunk, pair.shape),
-            per_chunk(chunk, 1, 256),
+            resident(embed.shape),
+            resident(time_weight.shape),
+            resident(shift_weight.shape),
             resident(inlet.shape),
             resident(kernel_one.shape),
             resident(small.shape),
         ],
-        out_specs=[per_chunk(chunk, *s[1:]) for s in shapes],
-        out_shape=[jax.ShapeDtypeStruct(s, jnp.float32) for s in shapes],
-        scratch_shapes=[pltpu.VMEM((chunk, 288, 768), jnp.bfloat16)],
+        out_specs=[per_chunk(chunk, *s[1:]) for s in shapes] + [resident((n, deep))] * 4,
+        out_shape=[jax.ShapeDtypeStruct(s, jnp.float32) for s in shapes]
+        + [jax.ShapeDtypeStruct((n, deep), kind) for kind in whole],
+        scratch_shapes=[
+            pltpu.VMEM((chunk, 288, 768), jnp.bfloat16),
+            pltpu.VMEM((n, 256), jnp.float32),
+        ],
         compiler_params=pltpu.CompilerParams(vmem_limit_bytes=VMEM_LIMIT),
         cost_estimate=pl.CostEstimate(
             flops=2 * n * 256 * 256 * 2400, bytes_accessed=n * 1 << 19, transcendentals=n * 1 << 16
         ),
         name="forward_part",
-    )(mix, pair, tshift, inlet, kernel_one, small)
+    )(mix, pair, embed, time_weight, shift_weight, inlet, kernel_one, small)
 
 
 def main_part(chunk, sizes, coef, start, inner, stats, noisy, target, keep, weights, small, bias_qkv, times):
@@ -1158,11 +1202,17 @@
 
     def update(k, rate, grad):
         weight = weights[k][...]
-        first, second = moments(states[k][0], states[k][1], grad * clip)
+        old = (states[k][0], states[k][1]) if k < 2 else (states[k][:, 0, :], states[k][:, 1, :])
+        first, second = moments(*old, grad * clip)
         firsts[k][...] = first
         seconds[k][...] = second
         step = first * scalars[0] / (jnp.sqrt(second * scalars[1]) + EPS_ADAM)
-        averaged(updated[k], (), weight - rate * (step + DECAY * weight), averages[k][...])
+        new = weight - rate * (step + DECAY * weight)
+        if k < 2:
+            averaged(updated[k], (), new, averages[k][...])
+        else:
+            updated[k][:, 0, :] = new
+            updated[k][:, 1, :] = kept * averages[k][...] + (1.0 - kept) * new
 
     update(0, RATES[3], jnp.concatenate([time_left[...], time_right[...]], axis=1))
     update(1, RATES[4], shift_rows[...])
@@ -1202,7 +1252,8 @@
         return pl.BlockSpec(lead + (part, wide), lambda b: (0,) * len(lead) + (b, 0))
 
     def five(lead):
-        return [rows_of(0, lead), rows_of(1, lead)] + [resident(lead + w.shape) for w in weights[2:]]
+        small = [w.shape[:1] + lead + w.shape[1:] for w in weights[2:]]
+        return [rows_of(0, lead), rows_of(1, lead)] + [resident(block) for block in small]
 
     shift_at = 2 * time_rows // shift_part
     rest_at = (2 * time_rows + shift_rows) // 256
@@ -1239,7 +1290,8 @@
             shape((2, 2, batch * tall, width)),
             shape((2, 4, batch * short, width)),
         ]
-        + [shape((2,) + w.shape) for w in weights]
+        + [shape((2,) + w.shape) for w in weights[:2]]
+        + [shape((w.shape[0], 2, w.shape[1])) for w in weights[2:]]
         + [shape(w.shape) for w in weights] * 2
         + [shape(state_kernel.shape[1:]), shape(state_attention.shape[1:])] * 2
         + [shape((1, 1))] * 2,
@@ -1297,67 +1349,36 @@
     width_sin = time_weight.shape[0] - time_weight.shape[1]
     rows, batch = lax.axis_size("rows"), lax.axis_size("batch")
     own = timesteps.shape[0] // rows
-    pair = jnp.concatenate([x_clean, noise], axis=1)
-    pair = pair.reshape(rows, own, 6, -1)
-    pair = jnp.pad(pair, ((0, 0), (0, 0), (0, 2), (0, 0)))
+    keep = keep_mask.reshape(rows, own, -1, chans).astype(jnp.bfloat16)
+    keep, timesteps, x_clean, noise = lax.optimization_barrier((keep, timesteps, x_clean, noise))
+    keep = lax.all_to_all(keep, "rows", 0, 0, tiled=True)
+    halves = [a.reshape(rows, own, 3, -1) for a in (x_clean, noise)]
+    pair = jnp.pad(jnp.concatenate(halves, axis=3), ((0, 0), (0, 0), (0, 1), (0, 0)))
     pair = lax.all_to_all(pair, "rows", 0, 0, tiled=True)
-    keep = keep_mask.reshape(rows, own, -1, chans).astype(jnp.bfloat16)
-    (
-        keep,
-        timesteps,
-        adam_step,
-        inlet_low,
-        kernels,
-        projections,
-        time_low,
-        shift_low,
-        outlet_low,
-        small_low,
-    ) = lax.optimization_barrier(
-        (
-            keep,
-            timesteps,
-            adam_step,
-            inlet_weight,
-            kernel_weight,
-            attention_weight,
-            time_weight,
-            shift_weight,
-            outlet_weight,
-            small_params,
-        )
-    )
-    keep = lax.all_to_all(keep, "rows", 0, 0, tiled=True)
+    pair, inlet_low, kernels, projections, outlet_low = lax.optimization_barrier(
+        (pair, inlet_weight, kernel_weight, attention_weight, outlet_weight)
+    )
     timesteps = lax.dynamic_slice_in_dim(timesteps, lax.axis_index("rows") * own, own, 0)
     bars = alpha_bars(timesteps)
     mix = jnp.stack([jnp.sqrt(bars), jnp.sqrt(1.0 - bars)])
     kernels = kernels.astype(jnp.bfloat16)
     projections = projections.astype(jnp.bfloat16)
-    time_low = time_low.astype(jnp.bfloat16)
-    shift_low = shift_low.astype(jnp.bfloat16)
     inlet = padded_taps(inlet_low).astype(jnp.bfloat16)
     outlet = padded_taps(
         jnp.transpose(outlet_low.reshape(3, 9, chans), (1, 0, 2)).reshape(27, chans)
     ).astype(jnp.bfloat16)
     qkv = jnp.concatenate([projections[0], projections[1], projections[2]], axis=1)
     embed = sinusoid(timesteps, width_sin).astype(jnp.bfloat16)
-    hidden_pre = jnp.dot(
-        embed, time_low[:width_sin], preferred_element_type=jnp.float32
-    ) + small_low[15:17].reshape(-1)
-    hidden = jax.nn.silu(hidden_pre).astype(jnp.bfloat16)
-    time_emb = jnp.dot(
-        hidden, time_low[width_sin:], preferred_element_type=jnp.float32
-    ) + small_low[17:19].reshape(-1)
-    time_act = jax.nn.silu(time_emb).astype(jnp.bfloat16)
-    time_shift = jnp.dot(time_act, shift_low, preferred_element_type=jnp.float32) + small_low[14]
     ratio = bars / (1.0 - bars)
     snr_weight = jnp.minimum(ratio, GAMMA) / ratio
     denom = 3 * 256 * own * rows * batch
     coef = 2.0 * snr_weight / denom
-    start, inner, stats, noisy, target = forward_part(
-        FORWARD_CHUNK, mix, pair, (time_shift + small_low[9])[:, None, :], inlet, kernels[0], small_low
-    )
-    bias_qkv = jnp.concatenate([small_low[11], jnp.zeros_like(small_low[0]), small_low[12]])
+    start, inner, stats, noisy, target, hidden, hidden_slope, time_act, time_slope = forward_part(
+        FORWARD_CHUNK, mix, pair, embed, time_weight, shift_weight, inlet, kernels[0], small_params
+    )
+    bias_qkv = jnp.concatenate(
+        [small_params[11], jnp.zeros_like(small_params[0]), small_params[12]]
+    )
     tall, short = state_kernel.shape[2], state_attention.shape[2]
     shard_rows = rows * padded_rows(2 * tall + 4 * short, rows)
     lanes = padded_rows(MISC_TOTAL, batch * rows)
@@ -1381,17 +1402,9 @@
             projections[3].T,
             outlet,
         ),
-        small_low,
+        small_params,
         bias_qkv[None],
-        (
-            embed,
-            hidden,
-            swish_grad(hidden_pre),
-            time_act,
-            swish_grad(time_emb),
-            time_low[width_sin:],
-            shift_low,
-        ),
+        (embed, hidden, hidden_slope, time_act, time_slope, time_weight, shift_weight),
     )
     count = adam_step[0].astype(jnp.float32)
     scalars = jnp.stack(
@@ -1421,11 +1434,13 @@
         state_attention,
         rest.reshape(-1, chans),
         (time_weight, shift_weight, inlet_weight, outlet_weight, small_params),
-        (state_time, state_shift, state_inlet, state_outlet, state_small),
+        (state_time, state_shift)
+        + tuple(jnp.transpose(a, (1, 0, 2)) for a in (state_inlet, state_outlet, state_small)),
         (average_time, average_shift, average_inlet, average_outlet, average_small),
     )
     kernel_pair, attention_pair = results[:2]
-    triples = [results[2 + 5 * k : 7 + 5 * k] for k in range(3)]
+    triples = [list(results[2 + 5 * k : 7 + 5 * k]) for k in range(3)]
+    triples[0][2:] = [jnp.transpose(a, (1, 0, 2)) for a in triples[0][2:]]
     first_conv, first_attention, second_conv, second_attention, loss, norm = results[17:]
     ordered = []
     for (time, shift, inlet, outlet, small), middle in zip(

time: 339 us -> 323 us (0.953)
  local copies, waits for them, and re-layouts: 28.2 us -> 14.3 us
  waiting for transfers between devices: 1.45 us -> 7.6 us
  other arithmetic: 17.6 us -> 13.9 us
    unnamed x54 -> x21, local copies, waits for them, and re-layouts: 11.9 us -> 1.7 us
    all_to_all x1, waiting for transfers between devices: 0.01 us -> 5.43 us  [local(): keep = lax.all_to_all(keep, 'rows', 0, 0, tiled=True)]
  transfers between devices with their start and end apart: 4 -> 4, of which waited for: 0 -> 2; matrix products, arithmetic and copies ran while one was open for 12% -> 8% of each run, Pallas kernels for 73% -> 76%
where the time goes in v2:
time: 323 us; the launch traced here: 322 us
  Pallas kernels  262 us (81%)
  between operations  15.1 us (5%)
  local copies, waits for them, and re-layouts  14.3 us (4%)
  other arithmetic  13.9 us (4%)
  starting transfers between devices  9.19 us (3%)
  waiting for transfers between devices  7.6 us (2%)
    pallas_call x1, Pallas kernels, main_part(): pl.pallas_call(functools.partial(second_kernel, tall, short), grid=(n //...  119 us
    pallas_call x1, Pallas kernels, exchange(): pl.pallas_call(functools.partial(exchange_kernel, (pairs, tall, quads, sh...  100 us
    pallas_call x1, Pallas kernels, forward_part(): pl.pallas_call(first_kernel, grid=(n // chunk,), in_specs=[pl.BlockSpec(m...  24.6 us
    pallas_call x1, Pallas kernels, finish(): pl.pallas_call(finish_kernel, grid=(batch,), in_specs=[pl.BlockSpec(memor...  17.9 us
    convert_element_type x1, other arithmetic, local(): keep = keep_mask.reshape(rows, own, -1, chans).astype(jnp.bfloat16)  6.72 us
  transfers between devices with their start and end apart: 4, of which 2 were waited for; matrix products, arithmetic and copies ran while one was open for 8% of the time, Pallas kernels for 76%

profile of v2, /device:TPU:1, one launch (start us, length us, event | category | flops | bytes accessed | tf_op | source)
XLA Modules:
  0.0 322.1 jit_solution(5458592452862610231)
XLA Ops:
  7.2 0.7 all-gather.5.cloned.1.call-update
  7.9 6.7 %convert_element_type.40 = bf16[128,4,16,256]{3,2,1,0:T(8,128)(2,1)} convert(s32[128,4,16,256]{3,2,1,0:T(8,128)} %param.30) | non-fusion elementwise | flops 2097152 | bytes 12582912 | tf_op jit(solution)/shard_map/convert_element_type | solution.py:1352
  15.6 0.9 select_maximum_fusion
  16.5 4.3 %all-to-all-start = ((f32[4,32,4,128]{3,2,1,0:T(4,128)}), f32[4,32,4,128]{3,2,1,0:T(4,128)S(1)}, u32[]{:S(2)}, u32[]{:S(2)}) async-start(f32[4,32,4,128]{3,2,1,0:T(4,128)} %select_maximum_fusion), calls=%async_computation | async-start | bytes 524288 | tf_op jit(solution)/shard_map/all_to_all | solution.py:1357
  20.7 0.7 all-gather.3.cloned.1.call-update
  21.5 0.8 fusion.6
  22.3 0.6 broadcast_in_dim.5.bias_qkv
  23.8 0.6 pad_maximum_fusion.4.scalars
  24.6 0.7 all-to-all-done.pair
  25.4 0.7 copy-done.2
  26.1 4.9 %all-to-all-start.1 = ((bf16[4,32,64,256]{3,2,1,0:T(8,128)(2,1)}), bf16[4,32,64,256]{3,2,1,0:T(8,128)(2,1)}, u32[]{:S(2)}, u32[]{:S(2)}) async-start(bf16[4,32,64,256]{3,2,1,0:T(8,128)(2,1)} %bitcast.62), calls=%async_computation.1 | async-start | bytes 8388608 | tf_op jit(solution)/shard_map/all_to_all | solution.py:1354
  31.5 0.6 pad_maximum_fusion.3.mix
  32.2 0.7 pad_maximum_fusion.1.embed
  32.9 2.7 convert_element_type.45
  35.6 1.0 copy.70
  36.6 1.7 fusion.5
  38.4 1.0 copy-done.1
  39.3 0.7 slice_bitcast_fusion.3
  40.0 0.8 fusion.3
  40.8 0.6 reshape.141
  41.4 0.9 copy.72.qkv
  42.4 0.8 copy.73.proj
  43.1 0.7 copy.69
  43.9 1.1 rev.7
  45.0 1.5 copy.68
  46.6 0.6 pad_bitcast_fusion.1.inlet
  47.2 0.6 pad_bitcast_fusion.outlet
  47.8 24.6 %forward_part.1 = (f32[32,256,256]{2,1,0:T(8,128)}, f32[32,256,256]{2,1,0:T(8,128)}, f32[32,8,256]{2,1,0:T(8,128)}, f32[32,8,256]{2,1,0:T(8,128)}, f32[32,8,256]...) custom-call(f32[2,32]{1,0:T(2,128)} %pad_maximum_fusion.3.mix, ...), custom_call_target="tpu_custom_call" | custom-call | flops 10066329600 | bytes 16777216 | tf_op jit(solution)/shard_map/forward_part/pallas_call | solution.py:614
  72.4 5.4 %all-to-all-done.1.keep = bf16[4,32,64,256]{3,2,1,0:T(8,128)(2,1)} async-done(((bf16[4,32,64,256]{3,2,1,0:T(8,128)(2,1)}), bf16[4,32,64,256]{3,2,1,0:T(8,128)(2,1)}, u32[]{:S(2)}, u32[]{:S(2)}) %all-to-all-start.1) | async-done | bytes 4194336 | tf_op jit(solution)/shard_map/all_to_all | solution.py:1354
  77.8 119.4 %main_part.1 = (f32[8,704,256]{2,1,0:T(8,128)}, f32[2048,256]{1,0:T(8,128)}) custom-call(f32[32]{0:T(128)} %get-tuple-element.135.coef, f32[32,256,256]{2,1,0:T(8,128)} %get-tuple-element.76.start_in, f32[32,256,256]{2,1,0:T(8,128)} %get-tuple-element.77.inner_in, f32[32,8,256]{2,1,0:T(8,128)} %get-tuple-element.78.stats_in, ...), custom_call_target="tpu_custom_call" | custom-call | flops 75161927680 | bytes 20971520 | tf_op jit(solution)/shard_map/main_part/pallas_call | solution.py:647
  197.2 100.0 %exchange.1 = (f32[4,2,2,2,176,256]{5,4,3,2,1,0:T(8,128)}, f32[4,2,2,2,64,256]{5,4,3,2,1,0:T(8,128)}, f32[4,176,256]{2,1,0:T(8,128)}, f32[8,128]{1,0:T(8,128)}) custom-call(f32[4,2,2,2,176,256]{5,4,3,2,1,0:T(8,128)} %bitcast.64, f32[4,2,2,2,64,256]{5,4,3,2,1,0:T(8,128)} %bitcast.67, f32[2,2,288,256]{3,2,1,0:T(8,128)} %state_kernel.3, ...), custom_call_target="tpu_custom_call" | custom-call | tf_op jit(solution)/shard_map/exchange/pallas_call | solution.py:1106
  297.3 17.9 %finish.1 = (f32[2,2,2304,256]{3,2,1,0:T(8,128)}, f32[2,4,256,256]{3,2,1,0:T(8,128)}, f32[2,640,512]{2,1,0:T(8,128)}, f32[2,512,256]{2,1,0:T(8,128)}, f32[27,2,2...) custom-call(f32[3]{0:T(128)} %pad_maximum_fusion.4.scalars, ...), custom_call_target="tpu_custom_call" | custom-call | flops 41943040 | bytes 37748736 | tf_op jit(solution)/shard_map/finish/pallas_call | solution.py:1260
  (38 shorter events, 2.1 us)
Async XLA Ops:
  7.2 290.1 %all-gather.5.cloned.1.call-start = ((), (), s32[]{:S(2)}) async-start(), calls=%async_computation.3 | async-start | bytes 1179648 | tf_op jit(solution)/shard_map/all_gather | solution.py:1431
  7.9 6.7 %copy-start.5 = (f32[128,3,4,16]{0,3,2,1:T(8,128)S(1)}, f32[128,3,4,16]{0,3,2,1:T(8,128)}, u32[]{:S(2)}) copy-start(f32[128,3,4,16]{0,3,2,1:T(8,128)} %param.27) | copy-start | bytes 294916
  7.9 7.2 %copy-start.6 = (f32[128,3,4,16]{0,3,2,1:T(8,128)S(1)}, f32[128,3,4,16]{0,3,2,1:T(8,128)}, u32[]{:S(2)}) copy-start(f32[128,3,4,16]{0,3,2,1:T(8,128)} %param.28) | copy-start | bytes 294916
  14.7 9.0 %copy-start.9 = (s32[128]{0:T(128)S(1)}, s32[128]{0:T(128)}, u32[]{:S(2)}) copy-start(s32[128]{0:T(128)} %param.29) | copy-start | bytes 1540
  14.7 9.8 %copy-start.8 = (f32[1000]{0:T(1024)S(1)}, f32[1000]{0:T(1024)}, u32[]{:S(2)}) copy-start(f32[1000]{0:T(1024)} %constant.59) | copy-start | bytes 12004
  16.5 8.9 %all-to-all-start = ((f32[4,32,4,128]{3,2,1,0:T(4,128)}), f32[4,32,4,128]{3,2,1,0:T(4,128)S(1)}, u32[]{:S(2)}, u32[]{:S(2)}) async-start(f32[4,32,4,128]{3,2,1,0:T(4,128)} %select_maximum_fusion), calls=%async_computation | async-start | bytes 524288 | tf_op jit(solution)/shard_map/all_to_all | solution.py:1357
  20.7 276.6 %all-gather.3.cloned.1.call-start = ((), (), s32[]{:S(2)}) async-start(), calls=%async_computation.2 | async-start | bytes 5308416 | tf_op jit(solution)/shard_map/all_gather | solution.py:1430
  25.4 0.7 copy-start.2
  26.1 51.7 %all-to-all-start.1 = ((bf16[4,32,64,256]{3,2,1,0:T(8,128)(2,1)}), bf16[4,32,64,256]{3,2,1,0:T(8,128)(2,1)}, u32[]{:S(2)}, u32[]{:S(2)}) async-start(bf16[4,32,64,256]{3,2,1,0:T(8,128)(2,1)} %bitcast.62), calls=%async_computation.1 | async-start | bytes 8388608 | tf_op jit(solution)/shard_map/all_to_all | solution.py:1354
  32.9 2.7 copy-start
  38.3 1.0 copy-start.1
  38.3 2.5 copy-start.4
  43.8 2.6 copy-start.3
  43.9 2.7 copy-start.7
Sparse Core Ops, SparseCore 0:
  9.6 24.5 all-gather.4
  35.9 51.2 all-gather.2

commit v3 on v2

--- a/solution.py
+++ b/solution.py
@@ -1354,7 +1354,15 @@
     keep = lax.all_to_all(keep, "rows", 0, 0, tiled=True)
     halves = [a.reshape(rows, own, 3, -1) for a in (x_clean, noise)]
     pair = jnp.pad(jnp.concatenate(halves, axis=3), ((0, 0), (0, 0), (0, 1), (0, 0)))
-    pair = lax.all_to_all(pair, "rows", 0, 0, tiled=True)
+    here = lax.axis_index("rows")
+    parts = [lax.dynamic_index_in_dim(pair, here, 0, keepdims=False)]
+    for d in range(1, rows):
+        block = lax.dynamic_index_in_dim(pair, (here + d) % rows, 0, keepdims=False)
+        parts.append(lax.ppermute(block, "rows", [(i, (i + d) % rows) for i in range(rows)]))
+    steps = ((here - jnp.arange(rows)) % rows)[:, None, None, None]
+    pair = jnp.broadcast_to(parts[0], (rows,) + parts[0].shape)
+    for d in range(1, rows):
+        pair = jnp.where(steps == d, parts[d], pair)
     pair, inlet_low, kernels, projections, outlet_low = lax.optimization_barrier(
         (pair, inlet_weight, kernel_weight, attention_weight, outlet_weight)
     )

time: 323 us -> 316 us (0.978)
  waiting for transfers between devices: 7.6 us -> 2.47 us
    all_to_all x1, waiting for transfers between devices: 5.43 us -> 1.05 us  [local(): keep = lax.all_to_all(keep, 'rows', 0, 0, tiled=True)]
    all_to_all x1 -> x0, starting transfers between devices: 4.27 us -> none  [local(): pair = lax.all_to_all(pair, 'rows', 0, 0, tiled=True)]
    ppermute x0 -> x3, starting transfers between devices: none -> 3.59 us  [local(): lax.ppermute(block, 'rows', [(i, (i + d) % rows) for i in range(rows)])]
  transfers between devices with their start and end apart: 4 -> 6, of which waited for: 2 -> 1; matrix products, arithmetic and copies ran while one was open for 8% -> 8% of each run, Pallas kernels for 76% -> 77%
where the time goes in v3:
time: 316 us
  Pallas kernels  262 us (83%)
  between operations  15.2 us (5%)
  other arithmetic  14 us (4%)
  local copies, waits for them, and re-layouts  13.1 us (4%)
  starting transfers between devices  8.53 us (3%)
    pallas_call x1, Pallas kernels, main_part(): pl.pallas_call(functools.partial(second_kernel, tall, short), grid=(n //...  119 us
    pallas_call x1, Pallas kernels, exchange(): pl.pallas_call(functools.partial(exchange_kernel, (pairs, tall, quads, sh...  100 us
    pallas_call x1, Pallas kernels, forward_part(): pl.pallas_call(first_kernel, grid=(n // chunk,), in_specs=[pl.BlockSpec(m...  24.6 us
    pallas_call x1, Pallas kernels, finish(): pl.pallas_call(finish_kernel, grid=(batch,), in_specs=[pl.BlockSpec(memor...  17.9 us
    convert_element_type x1, other arithmetic, local(): keep = keep_mask.reshape(rows, own, -1, chans).astype(jnp.bfloat16)  6.71 us
  transfers between devices with their start and end apart: 6, of which 1 were waited for; matrix products, arithmetic and copies ran while one was open for 8% of the time, Pallas kernels for 77%

profile of v3, /device:TPU:1, one launch (start us, length us, event | category | flops | bytes accessed | tf_op | source)
XLA Modules:
  0.0 315.7 jit_solution(943012162092774444)
XLA Ops:
  7.2 0.7 all-gather.5.cloned.1.call-update
  8.0 6.7 %convert_element_type.40 = bf16[128,4,16,256]{3,2,1,0:T(8,128)(2,1)} convert(s32[128,4,16,256]{3,2,1,0:T(8,128)} %param.30) | non-fusion elementwise | flops 2097152 | bytes 12582912 | tf_op jit(solution)/shard_map/convert_element_type | solution.py:1352
  15.7 3.0 collective-permute-start
  18.7 0.2 collective-permute-start.1
  19.0 0.3 collective-permute-start.2
  19.3 4.9 %all-to-all-start = ((bf16[4,32,64,256]{3,2,1,0:T(8,128)(2,1)}), bf16[4,32,64,256]{3,2,1,0:T(8,128)(2,1)}, u32[]{:S(2)}, u32[]{:S(2)}) async-start(bf16[4,32,64,256]{3,2,1,0:T(8,128)(2,1)} %bitcast.70), calls=%async_computation | async-start | bytes 8388608 | tf_op jit(solution)/shard_map/all_to_all | solution.py:1354
  24.2 0.7 all-gather.3.cloned.1.call-update
  25.3 0.5 sqrt_bitcast_fusion.1
  25.8 0.8 fusion.7
  26.6 0.6 broadcast_in_dim.50.bias_qkv
  28.0 0.6 pad_maximum_fusion.3.mix
  28.8 0.7 pad_maximum_fusion.1.embed
  29.4 0.6 pad_maximum_fusion.4.scalars
  30.3 0.8 select_select_fusion.pair
  31.1 2.7 convert_element_type.45
  33.8 1.0 copy.100
  34.8 1.7 fusion.6
  36.6 1.0 copy-done.1
  37.5 0.7 slice_bitcast_fusion.3
  38.2 0.8 fusion.4
  39.1 0.9 copy.102.qkv
  40.0 1.5 copy.98
  41.5 0.7 copy.99
  42.2 1.1 rev.7
  43.3 0.8 copy.103.proj
  44.1 0.6 pad_bitcast_fusion.1.inlet
  44.8 0.6 pad_bitcast_fusion.outlet
  45.4 24.6 %forward_part.1 = (f32[32,256,256]{2,1,0:T(8,128)}, f32[32,256,256]{2,1,0:T(8,128)}, f32[32,8,256]{2,1,0:T(8,128)}, f32[32,8,256]{2,1,0:T(8,128)}, f32[32,8,256]...) custom-call(f32[2,32]{1,0:T(2,128)} %pad_maximum_fusion.3.mix, ...), custom_call_target="tpu_custom_call" | custom-call | flops 10066329600 | bytes 16777216 | tf_op jit(solution)/shard_map/forward_part/pallas_call | solution.py:614
  70.0 1.0 all-to-all-done.keep
  71.0 119.4 %main_part.1 = (f32[8,704,256]{2,1,0:T(8,128)}, f32[2048,256]{1,0:T(8,128)}) custom-call(f32[32]{0:T(128)} %get-tuple-element.139.coef, f32[32,256,256]{2,1,0:T(8,128)} %get-tuple-element.76.start_in, f32[32,256,256]{2,1,0:T(8,128)} %get-tuple-element.77.inner_in, f32[32,8,256]{2,1,0:T(8,128)} %get-tuple-element.78.stats_in, ...), custom_call_target="tpu_custom_call" | custom-call | flops 75161927680 | bytes 20971520 | tf_op jit(solution)/shard_map/main_part/pallas_call | solution.py:647
  190.5 100.4 %exchange.1 = (f32[4,2,2,2,176,256]{5,4,3,2,1,0:T(8,128)}, f32[4,2,2,2,64,256]{5,4,3,2,1,0:T(8,128)}, f32[4,176,256]{2,1,0:T(8,128)}, f32[8,128]{1,0:T(8,128)}) custom-call(f32[4,2,2,2,176,256]{5,4,3,2,1,0:T(8,128)} %bitcast.72, f32[4,2,2,2,64,256]{5,4,3,2,1,0:T(8,128)} %bitcast.75, f32[2,2,288,256]{3,2,1,0:T(8,128)} %state_kernel.3, ...), custom_call_target="tpu_custom_call" | custom-call | tf_op jit(solution)/shard_map/exchange/pallas_call | solution.py:1106
  290.9 17.9 %finish.1 = (f32[2,2,2304,256]{3,2,1,0:T(8,128)}, f32[2,4,256,256]{3,2,1,0:T(8,128)}, f32[2,640,512]{2,1,0:T(8,128)}, f32[2,512,256]{2,1,0:T(8,128)}, f32[27,2,2...) custom-call(f32[3]{0:T(128)} %pad_maximum_fusion.4.scalars, ...), custom_call_target="tpu_custom_call" | custom-call | flops 41943040 | bytes 37748736 | tf_op jit(solution)/shard_map/finish/pallas_call | solution.py:1260
  (46 shorter events, 1.9 us)
Async XLA Ops:
  7.2 283.7 %all-gather.5.cloned.1.call-start = ((), (), s32[]{:S(2)}) async-start(), calls=%async_computation.2 | async-start | bytes 1179648 | tf_op jit(solution)/shard_map/all_gather | solution.py:1439
  8.0 6.7 %copy-start.4 = (f32[128,3,4,16]{0,3,2,1:T(8,128)S(1)}, f32[128,3,4,16]{0,3,2,1:T(8,128)}, u32[]{:S(2)}) copy-start(f32[128,3,4,16]{0,3,2,1:T(8,128)} %param.27) | copy-start | bytes 294916
  8.0 7.1 %copy-start.5 = (f32[128,3,4,16]{0,3,2,1:T(8,128)S(1)}, f32[128,3,4,16]{0,3,2,1:T(8,128)}, u32[]{:S(2)}) copy-start(f32[128,3,4,16]{0,3,2,1:T(8,128)} %param.28) | copy-start | bytes 294916
  15.7 14.4 %collective-permute-start = (f32[32,4,128]{2,0,1:T(8,128)S(1)}, f32[32,4,128]{2,0,1:T(8,128)S(1)}, u32[]{:S(2)}, u32[]{:S(2)}) collective-permute-start(f32[32,4,128]{2,0,1:T(8,128)S(1)} %get-tuple-element.130), channel_id=1, source_target_pairs={{0,3},{1,0},{2,1},{3,2},{4,7},{5,4},{6,5},{7,6},{8,11},{9,8},{10,9... | collective-permute-start | bytes 196616 | tf_op jit(solution)/shard_map/ppermute | solution.py:1361
  18.7 11.4 %collective-permute-start.1 = (f32[32,4,128]{2,0,1:T(8,128)S(1)}, f32[32,4,128]{2,0,1:T(8,128)S(1)}, u32[]{:S(2)}, u32[]{:S(2)}) collective-permute-start(f32[32,4,128]{2,0,1:T(8,128)S(1)} %get-tuple-element.132), channel_id=1, source_target_pairs={{0,2},{1,3},{2,0},{3,1},{4,6},{5,7},{6,4},{7,5},{8,10},{9,11},{10,... | collective-permute-start | bytes 196616 | tf_op jit(solution)/shard_map/ppermute | solution.py:1361
  18.9 6.0 %copy-start.7 = (s32[128]{0:T(128)S(1)}, s32[128]{0:T(128)}, u32[]{:S(2)}) copy-start(s32[128]{0:T(128)} %param.29) | copy-start | bytes 1540
  19.0 6.1 %copy-start.6 = (f32[1000]{0:T(1024)S(1)}, f32[1000]{0:T(1024)}, u32[]{:S(2)}) copy-start(f32[1000]{0:T(1024)} %constant.105) | copy-start | bytes 12004
  19.0 11.2 %collective-permute-start.2 = (f32[32,4,128]{2,0,1:T(8,128)S(1)}, f32[32,4,128]{2,0,1:T(8,128)S(1)}, u32[]{:S(2)}, u32[]{:S(2)}) collective-permute-start(f32[32,4,128]{2,0,1:T(8,128)S(1)} %get-tuple-element.131), channel_id=1, source_target_pairs={{0,1},{1,2},{2,3},{3,0},{4,5},{5,6},{6,7},{7,4},{8,9},{9,10},{10,1... | collective-permute-start | bytes 196616 | tf_op jit(solution)/shard_map/ppermute | solution.py:1361
  19.3 51.7 %all-to-all-start = ((bf16[4,32,64,256]{3,2,1,0:T(8,128)(2,1)}), bf16[4,32,64,256]{3,2,1,0:T(8,128)(2,1)}, u32[]{:S(2)}, u32[]{:S(2)}) async-start(bf16[4,32,64,256]{3,2,1,0:T(8,128)(2,1)} %bitcast.70), calls=%async_computation | async-start | bytes 8388608 | tf_op jit(solution)/shard_map/all_to_all | solution.py:1354
  24.1 266.8 %all-gather.3.cloned.1.call-start = ((), (), s32[]{:S(2)}) async-start(), calls=%async_computation.1 | async-start | bytes 5308416 | tf_op jit(solution)/shard_map/all_gather | solution.py:1438
  31.1 2.7 copy-start
  36.5 1.0 copy-start.1
  36.5 2.5 copy-start.3
  41.5 2.6 copy-start.2
Sparse Core Ops, SparseCore 0:
  9.6 24.5 all-gather.4
  35.9 51.2 all-gather.2

commit v4 on v3

--- a/solution.py
+++ b/solution.py
@@ -12,7 +12,6 @@
 G = 32
 
 
-HIGH_PRECISION = lax.Precision.HIGHEST
 CLIP = 0.05
 GAMMA = 5.0
 KEEP = 0.9
@@ -45,11 +44,6 @@
     rates = jnp.exp(-math.log(10000.0) * jnp.arange(half).astype(jnp.float32) / (half - 1))
     angles = timesteps.astype(jnp.float32)[:, None] * rates[None, :]
     return jnp.concatenate([jnp.sin(angles), jnp.cos(angles)], axis=1)
-
-
-def swish_grad(pre):
-    logistic = jax.nn.sigmoid(pre)
-    return logistic * (1.0 + pre * (1.0 - logistic))
 
 
 def wrap(shift, size):
@@ -535,12 +529,12 @@
                 (shard_out.shape[0], shard_out.shape[1] - used, 256), jnp.float32
             )
         total = tshift_grad[...]
-        shift_grad = full_dot(time_act[...], total, TN)
-        grad_act = full_dot(total, shift_weight[...].astype(jnp.bfloat16), NT) * time_slope[...]
-        two_grad = full_dot(hidden[...], grad_act, TN)
+        shift_grad = rows_dot(time_act[...], total)
+        grad_act = back_dot(total, shift_weight[...].astype(jnp.bfloat16)) * time_slope[...]
+        two_grad = rows_dot(hidden[...], grad_act)
         time_two = time_weight[embed.shape[1] :, :].astype(jnp.bfloat16)
-        grad_hidden = full_dot(grad_act, time_two, NT) * hidden_slope[...]
-        one_grad = full_dot(embed[...], grad_hidden, TN)
+        grad_hidden = back_dot(grad_act, time_two) * hidden_slope[...]
+        one_grad = rows_dot(embed[...], grad_hidden)
         width = one_grad.shape[0]
         height = width + two_grad.shape[0]
         for half in range(2):
@@ -584,14 +578,21 @@
     return parts
 
 
-def full_dot(a, b, dims):
-    return lax.dot_general(
-        a.astype(jnp.float32),
-        b.astype(jnp.float32),
-        (dims, ((), ())),
-        precision=HIGH_PRECISION,
-        preferred_element_type=jnp.float32,
-    )
+def thirds(x):
+    high = x.astype(jnp.bfloat16).astype(jnp.float32)
+    middle = (x - high).astype(jnp.bfloat16).astype(jnp.float32)
+    return jnp.concatenate([high, middle, x - high - middle], axis=0).astype(jnp.bfloat16)
+
+
+def rows_dot(low, x):
+    wide = low.astype(jnp.float32)
+    return dot(jnp.concatenate([wide] * 3, axis=0).astype(jnp.bfloat16), thirds(x), TN)
+
+
+def back_dot(x, weight):
+    n = x.shape[0]
+    parts = dot(thirds(x), weight, NT)
+    return parts[0:n] + (parts[n : 2 * n] + parts[2 * n :])
 
 
 def resident(shape):
@@ -1012,12 +1013,6 @@
     square_copies = begin(
         [remote(square_core.at[0], square_core.at[1], square_send.at[0], square_recv.at[0], (partner, r))]
     )
-    shard_copies = begin(
-        [
-            remote(shard_grad.at[r], shard_grad.at[r], shard_send.at[d], shard_recv.at[d], (batch, peer))
-            for d, peer in enumerate(row_peers)
-        ]
-    )
     arrived(square_copies)
     square_rows[r] = square_core[0] + square_core[1]
     copies = begin(
@@ -1029,6 +1024,12 @@
                 square_recv.at[1 + d],
                 (batch, peer),
             )
+            for d, peer in enumerate(row_peers)
+        ]
+    )
+    shard_copies = begin(
+        [
+            remote(shard_grad.at[r], shard_grad.at[r], shard_send.at[d], shard_recv.at[d], (batch, peer))
             for d, peer in enumerate(row_peers)
         ]
     )

time: 316 us -> 314 us (level)
  no operation moved by 1% of the time
where the time goes in v4:
time: 314 us
  Pallas kernels  260 us (83%)
  between operations  15.2 us (5%)
  other arithmetic  14 us (4%)
  local copies, waits for them, and re-layouts  13.1 us (4%)
  starting transfers between devices  8.53 us (3%)
    pallas_call x1, Pallas kernels, main_part(): pl.pallas_call(functools.partial(second_kernel, tall, short), grid=(n //...  117 us
    pallas_call x1, Pallas kernels, exchange(): pl.pallas_call(functools.partial(exchange_kernel, (pairs, tall, quads, sh...  100 us
    pallas_call x1, Pallas kernels, forward_part(): pl.pallas_call(first_kernel, grid=(n // chunk,), in_specs=[pl.BlockSpec(m...  24.6 us
    pallas_call x1, Pallas kernels, finish(): pl.pallas_call(finish_kernel, grid=(batch,), in_specs=[pl.BlockSpec(memor...  17.9 us
    convert_element_type x1, other arithmetic, local(): keep = keep_mask.reshape(rows, own, -1, chans).astype(jnp.bfloat16)  6.71 us
  transfers between devices with their start and end apart: 6, of which 1 were waited for; matrix products, arithmetic and copies ran while one was open for 8% of the time, Pallas kernels for 77%

profile of v4, /device:TPU:1, one launch (start us, length us, event | category | flops | bytes accessed | tf_op | source)
XLA Modules:
  0.0 313.6 jit_solution(12044131981767538526)
XLA Ops:
  7.2 0.7 all-gather.5.cloned.1.call-update
  8.0 6.7 %convert_element_type.40 = bf16[128,4,16,256]{3,2,1,0:T(8,128)(2,1)} convert(s32[128,4,16,256]{3,2,1,0:T(8,128)} %param.30) | non-fusion elementwise | flops 2097152 | bytes 12582912 | tf_op jit(solution)/shard_map/convert_element_type | solution.py:1353
  15.7 3.0 collective-permute-start
  18.7 0.2 collective-permute-start.1
  19.0 0.3 collective-permute-start.2
  19.3 4.9 %all-to-all-start = ((bf16[4,32,64,256]{3,2,1,0:T(8,128)(2,1)}), bf16[4,32,64,256]{3,2,1,0:T(8,128)(2,1)}, u32[]{:S(2)}, u32[]{:S(2)}) async-start(bf16[4,32,64,256]{3,2,1,0:T(8,128)(2,1)} %bitcast.70), calls=%async_computation | async-start | bytes 8388608 | tf_op jit(solution)/shard_map/all_to_all | solution.py:1355
  24.2 0.7 all-gather.3.cloned.1.call-update
  25.3 0.5 sqrt_bitcast_fusion.1
  25.8 0.8 fusion.7
  26.6 0.6 broadcast_in_dim.50.bias_qkv
  28.0 0.6 pad_maximum_fusion.3.mix
  28.8 0.7 pad_maximum_fusion.1.embed
  29.4 0.6 pad_maximum_fusion.4.scalars
  30.3 0.8 select_select_fusion.pair
  31.1 2.7 convert_element_type.45
  33.8 1.0 copy.100
  34.8 1.7 fusion.6
  36.6 1.0 copy-done.1
  37.5 0.7 slice_bitcast_fusion.3
  38.2 0.8 fusion.4
  39.1 0.9 copy.102.qkv
  40.0 1.5 copy.98
  41.5 0.7 copy.99
  42.2 1.1 rev.7
  43.3 0.8 copy.103.proj
  44.1 0.6 pad_bitcast_fusion.1.inlet
  44.8 0.6 pad_bitcast_fusion.outlet
  45.4 24.6 %forward_part.1 = (f32[32,256,256]{2,1,0:T(8,128)}, f32[32,256,256]{2,1,0:T(8,128)}, f32[32,8,256]{2,1,0:T(8,128)}, f32[32,8,256]{2,1,0:T(8,128)}, f32[32,8,256]...) custom-call(f32[2,32]{1,0:T(2,128)} %pad_maximum_fusion.3.mix, ...), custom_call_target="tpu_custom_call" | custom-call | flops 10066329600 | bytes 16777216 | tf_op jit(solution)/shard_map/forward_part/pallas_call | solution.py:615
  70.0 1.0 all-to-all-done.keep
  71.0 117.3 %main_part.1 = (f32[8,704,256]{2,1,0:T(8,128)}, f32[2048,256]{1,0:T(8,128)}) custom-call(f32[32]{0:T(128)} %get-tuple-element.139.coef, f32[32,256,256]{2,1,0:T(8,128)} %get-tuple-element.76.start_in, f32[32,256,256]{2,1,0:T(8,128)} %get-tuple-element.77.inner_in, f32[32,8,256]{2,1,0:T(8,128)} %get-tuple-element.78.stats_in, ...), custom_call_target="tpu_custom_call" | custom-call | flops 75161927680 | bytes 20971520 | tf_op jit(solution)/shard_map/main_part/pallas_call | solution.py:648
  188.3 100.4 %exchange.1 = (f32[4,2,2,2,176,256]{5,4,3,2,1,0:T(8,128)}, f32[4,2,2,2,64,256]{5,4,3,2,1,0:T(8,128)}, f32[4,176,256]{2,1,0:T(8,128)}, f32[8,128]{1,0:T(8,128)}) custom-call(f32[4,2,2,2,176,256]{5,4,3,2,1,0:T(8,128)} %bitcast.72, f32[4,2,2,2,64,256]{5,4,3,2,1,0:T(8,128)} %bitcast.75, f32[2,2,288,256]{3,2,1,0:T(8,128)} %state_kernel.3, ...), custom_call_target="tpu_custom_call" | custom-call | tf_op jit(solution)/shard_map/exchange/pallas_call | solution.py:1107
  288.8 17.9 %finish.1 = (f32[2,2,2304,256]{3,2,1,0:T(8,128)}, f32[2,4,256,256]{3,2,1,0:T(8,128)}, f32[2,640,512]{2,1,0:T(8,128)}, f32[2,512,256]{2,1,0:T(8,128)}, f32[27,2,2...) custom-call(f32[3]{0:T(128)} %pad_maximum_fusion.4.scalars, ...), custom_call_target="tpu_custom_call" | custom-call | flops 41943040 | bytes 37748736 | tf_op jit(solution)/shard_map/finish/pallas_call | solution.py:1261
  (46 shorter events, 1.9 us)
Async XLA Ops:
  7.2 281.6 %all-gather.5.cloned.1.call-start = ((), (), s32[]{:S(2)}) async-start(), calls=%async_computation.2 | async-start | bytes 1179648 | tf_op jit(solution)/shard_map/all_gather | solution.py:1440
  8.0 6.7 %copy-start.4 = (f32[128,3,4,16]{0,3,2,1:T(8,128)S(1)}, f32[128,3,4,16]{0,3,2,1:T(8,128)}, u32[]{:S(2)}) copy-start(f32[128,3,4,16]{0,3,2,1:T(8,128)} %param.27) | copy-start | bytes 294916
  8.0 7.1 %copy-start.5 = (f32[128,3,4,16]{0,3,2,1:T(8,128)S(1)}, f32[128,3,4,16]{0,3,2,1:T(8,128)}, u32[]{:S(2)}) copy-start(f32[128,3,4,16]{0,3,2,1:T(8,128)} %param.28) | copy-start | bytes 294916
  15.7 14.4 %collective-permute-start = (f32[32,4,128]{2,0,1:T(8,128)S(1)}, f32[32,4,128]{2,0,1:T(8,128)S(1)}, u32[]{:S(2)}, u32[]{:S(2)}) collective-permute-start(f32[32,4,128]{2,0,1:T(8,128)S(1)} %get-tuple-element.130), channel_id=1, source_target_pairs={{0,3},{1,0},{2,1},{3,2},{4,7},{5,4},{6,5},{7,6},{8,11},{9,8},{10,9... | collective-permute-start | bytes 196616 | tf_op jit(solution)/shard_map/ppermute | solution.py:1362
  18.7 11.4 %collective-permute-start.1 = (f32[32,4,128]{2,0,1:T(8,128)S(1)}, f32[32,4,128]{2,0,1:T(8,128)S(1)}, u32[]{:S(2)}, u32[]{:S(2)}) collective-permute-start(f32[32,4,128]{2,0,1:T(8,128)S(1)} %get-tuple-element.132), channel_id=1, source_target_pairs={{0,2},{1,3},{2,0},{3,1},{4,6},{5,7},{6,4},{7,5},{8,10},{9,11},{10,... | collective-permute-start | bytes 196616 | tf_op jit(solution)/shard_map/ppermute | solution.py:1362
  18.9 6.0 %copy-start.7 = (s32[128]{0:T(128)S(1)}, s32[128]{0:T(128)}, u32[]{:S(2)}) copy-start(s32[128]{0:T(128)} %param.29) | copy-start | bytes 1540
  19.0 6.1 %copy-start.6 = (f32[1000]{0:T(1024)S(1)}, f32[1000]{0:T(1024)}, u32[]{:S(2)}) copy-start(f32[1000]{0:T(1024)} %constant.105) | copy-start | bytes 12004
  19.0 11.2 %collective-permute-start.2 = (f32[32,4,128]{2,0,1:T(8,128)S(1)}, f32[32,4,128]{2,0,1:T(8,128)S(1)}, u32[]{:S(2)}, u32[]{:S(2)}) collective-permute-start(f32[32,4,128]{2,0,1:T(8,128)S(1)} %get-tuple-element.131), channel_id=1, source_target_pairs={{0,1},{1,2},{2,3},{3,0},{4,5},{5,6},{6,7},{7,4},{8,9},{9,10},{10,1... | collective-permute-start | bytes 196616 | tf_op jit(solution)/shard_map/ppermute | solution.py:1362
  19.3 51.7 %all-to-all-start = ((bf16[4,32,64,256]{3,2,1,0:T(8,128)(2,1)}), bf16[4,32,64,256]{3,2,1,0:T(8,128)(2,1)}, u32[]{:S(2)}, u32[]{:S(2)}) async-start(bf16[4,32,64,256]{3,2,1,0:T(8,128)(2,1)} %bitcast.70), calls=%async_computation | async-start | bytes 8388608 | tf_op jit(solution)/shard_map/all_to_all | solution.py:1355
  24.1 264.7 %all-gather.3.cloned.1.call-start = ((), (), s32[]{:S(2)}) async-start(), calls=%async_computation.1 | async-start | bytes 5308416 | tf_op jit(solution)/shard_map/all_gather | solution.py:1439
  31.1 2.7 copy-start
  36.5 1.0 copy-start.1
  36.5 2.5 copy-start.3
  41.5 2.6 copy-start.2
Sparse Core Ops, SparseCore 0:
  9.6 24.5 all-gather.4
  35.9 51.2 all-gather.2

commit v5 on v4

--- a/solution.py
+++ b/solution.py
@@ -24,6 +24,7 @@
 VMEM_LIMIT = 60 << 20
 CHUNK = 4
 FORWARD_CHUNK = 8
+SHARDS = 4
 GROUP = 2
 COUNT = 2048.0
 RATES = (0.1, 0.01, 0.03, 0.05, 0.02, 0.01, 0.2)
@@ -1192,11 +1193,14 @@
         out[(1,) + index] = kept * average + (1.0 - kept) * new
 
     tall, short = state_kernel.shape[2], state_attention.shape[2]
-    for k in range(2):
-        averaged(kernel_out, (k,), fresh[0, k * tall : k * tall + tall], average_kernel[k])
-    for k in range(4):
-        at = 2 * tall + k * short
-        averaged(attention_out, (k,), fresh[0, at : at + short], average_attention[k])
+    for i in range(fresh.shape[0]):
+        for k in range(2):
+            place = (k, slice(i * tall, i * tall + tall))
+            averaged(kernel_out, place, fresh[i, k * tall : k * tall + tall], average_kernel[place])
+        for k in range(4):
+            place = (k, slice(i * short, i * short + short))
+            at = 2 * tall + k * short
+            averaged(attention_out, place, fresh[i, at : at + short], average_attention[place])
 
     def moments(first, second, g):
         return BETA_ONE * first + (1.0 - BETA_ONE) * g, BETA_TWO * second + (1.0 - BETA_TWO) * g * g
@@ -1242,7 +1246,8 @@
     batch, shard_rows, width = fresh.shape
     tall, short = state_kernel.shape[2], state_attention.shape[2]
     (time_rows, time_width), (shift_rows, _) = weights[0].shape, weights[1].shape
-    time_part, shift_part = time_rows // batch, shift_rows // batch
+    steps = batch // SHARDS
+    time_part, shift_part = time_rows // steps, shift_rows // steps
     shape = functools.partial(jax.ShapeDtypeStruct, dtype=jnp.float32)
 
     def at(block, index):
@@ -1260,18 +1265,18 @@
     rest_at = (2 * time_rows + shift_rows) // 256
     return pl.pallas_call(
         finish_kernel,
-        grid=(batch,),
+        grid=(steps,),
         in_specs=[
             pl.BlockSpec(memory_space=pltpu.SMEM),
             resident(norm_tile.shape),
-            at((1, shard_rows, width), lambda b: (b, 0, 0)),
-            at((2, tall, width), lambda b: (0, b, 0)),
-            at((4, short, width), lambda b: (0, b, 0)),
+            at((SHARDS, shard_rows, width), lambda b: (b, 0, 0)),
+            at((2, SHARDS * tall, width), lambda b: (0, b, 0)),
+            at((4, SHARDS * short, width), lambda b: (0, b, 0)),
             resident(shard_grad.shape),
             resident(state_kernel.shape),
             resident(state_attention.shape),
             at((time_part, width), lambda b: (b, 0)),
-            at((time_part, width), lambda b: (batch + b, 0)),
+            at((time_part, width), lambda b: (steps + b, 0)),
             at((shift_part, width), lambda b: (shift_at + b, 0)),
             pl.BlockSpec((256, width), lambda b: (rest_at, 0), pipeline_mode=pl.Buffered(1)),
         ]
@@ -1279,8 +1284,8 @@
         + five((2,))
         + five(()),
         out_specs=[
-            at((2, 2, tall, width), lambda b: (0, 0, b, 0)),
-            at((2, 4, short, width), lambda b: (0, 0, b, 0)),
+            at((2, 2, SHARDS * tall, width), lambda b: (0, 0, b, 0)),
+            at((2, 4, SHARDS * short, width), lambda b: (0, 0, b, 0)),
         ]
         + five((2,))
         + five(())

time: 314 us -> 311 us (level)
  transfers between devices with their start and end apart: 6 -> 6, of which waited for: 1 -> 1; matrix products, arithmetic and copies ran while one was open for 8% -> 8% of each run, Pallas kernels for 77% -> 78%
where the time goes in v5:
time: 311 us; the launch traced here: 310 us
  Pallas kernels  257 us (83%)
  between operations  15.2 us (5%)
  other arithmetic  14 us (5%)
  local copies, waits for them, and re-layouts  13.1 us (4%)
  starting transfers between devices  8.53 us (3%)
    pallas_call x1, Pallas kernels, main_part(): pl.pallas_call(functools.partial(second_kernel, tall, short), grid=(n //...  117 us
    pallas_call x1, Pallas kernels, exchange(): pl.pallas_call(functools.partial(exchange_kernel, (pairs, tall, quads, sh...  100 us
    pallas_call x1, Pallas kernels, forward_part(): pl.pallas_call(first_kernel, grid=(n // chunk,), in_specs=[pl.BlockSpec(m...  24.6 us
    pallas_call x1, Pallas kernels, finish(): pl.pallas_call(finish_kernel, grid=(steps,), in_specs=[pl.BlockSpec(memor...  14.8 us
    convert_element_type x1, other arithmetic, local(): keep = keep_mask.reshape(rows, own, -1, chans).astype(jnp.bfloat16)  6.71 us
  transfers between devices with their start and end apart: 6, of which 1 were waited for; matrix products, arithmetic and copies ran while one was open for 8% of the time, Pallas kernels for 78%

profile of v5, /device:TPU:1, one launch (start us, length us, event | category | flops | bytes accessed | tf_op | source)
XLA Modules:
  0.0 310.5 jit_solution(7440354649896666880)
XLA Ops:
  7.2 0.7 all-gather.5.cloned.1.call-update
  8.0 6.7 %convert_element_type.40 = bf16[128,4,16,256]{3,2,1,0:T(8,128)(2,1)} convert(s32[128,4,16,256]{3,2,1,0:T(8,128)} %param.30) | non-fusion elementwise | flops 2097152 | bytes 12582912 | tf_op jit(solution)/shard_map/convert_element_type | solution.py:1358
  15.7 3.0 collective-permute-start
  18.7 0.2 collective-permute-start.1
  19.0 0.3 collective-permute-start.2
  19.3 4.9 %all-to-all-start = ((bf16[4,32,64,256]{3,2,1,0:T(8,128)(2,1)}), bf16[4,32,64,256]{3,2,1,0:T(8,128)(2,1)}, u32[]{:S(2)}, u32[]{:S(2)}) async-start(bf16[4,32,64,256]{3,2,1,0:T(8,128)(2,1)} %bitcast.70), calls=%async_computation | async-start | bytes 8388608 | tf_op jit(solution)/shard_map/all_to_all | solution.py:1360
  24.2 0.7 all-gather.3.cloned.1.call-update
  25.3 0.5 sqrt_bitcast_fusion.1
  25.8 0.8 fusion.7
  26.6 0.6 broadcast_in_dim.50.bias_qkv
  28.0 0.6 pad_maximum_fusion.3.mix
  28.8 0.7 pad_maximum_fusion.1.embed
  29.4 0.6 pad_maximum_fusion.4.scalars
  30.3 0.8 select_select_fusion.pair
  31.1 2.7 convert_element_type.45
  33.8 1.0 copy.100
  34.8 1.7 fusion.6
  36.6 1.0 copy-done.1
  37.5 0.7 slice_bitcast_fusion.3
  38.2 0.8 fusion.4
  39.1 0.9 copy.102.qkv
  40.0 1.5 copy.98
  41.5 0.7 copy.99
  42.2 1.1 rev.7
  43.3 0.8 copy.103.proj
  44.1 0.6 pad_bitcast_fusion.1.inlet
  44.8 0.6 pad_bitcast_fusion.outlet
  45.4 24.6 %forward_part.1 = (f32[32,256,256]{2,1,0:T(8,128)}, f32[32,256,256]{2,1,0:T(8,128)}, f32[32,8,256]{2,1,0:T(8,128)}, f32[32,8,256]{2,1,0:T(8,128)}, f32[32,8,256]...) custom-call(f32[2,32]{1,0:T(2,128)} %pad_maximum_fusion.3.mix, ...), custom_call_target="tpu_custom_call" | custom-call | flops 10066329600 | bytes 16777216 | tf_op jit(solution)/shard_map/forward_part/pallas_call | solution.py:616
  70.0 1.0 all-to-all-done.keep
  71.0 117.3 %main_part.1 = (f32[8,704,256]{2,1,0:T(8,128)}, f32[2048,256]{1,0:T(8,128)}) custom-call(f32[32]{0:T(128)} %get-tuple-element.139.coef, f32[32,256,256]{2,1,0:T(8,128)} %get-tuple-element.76.start_in, f32[32,256,256]{2,1,0:T(8,128)} %get-tuple-element.77.inner_in, f32[32,8,256]{2,1,0:T(8,128)} %get-tuple-element.78.stats_in, ...), custom_call_target="tpu_custom_call" | custom-call | flops 75161927680 | bytes 20971520 | tf_op jit(solution)/shard_map/main_part/pallas_call | solution.py:649
  188.3 100.4 %exchange.1 = (f32[4,2,2,2,176,256]{5,4,3,2,1,0:T(8,128)}, f32[4,2,2,2,64,256]{5,4,3,2,1,0:T(8,128)}, f32[4,176,256]{2,1,0:T(8,128)}, f32[8,128]{1,0:T(8,128)}) custom-call(f32[4,2,2,2,176,256]{5,4,3,2,1,0:T(8,128)} %bitcast.72, f32[4,2,2,2,64,256]{5,4,3,2,1,0:T(8,128)} %bitcast.75, f32[2,2,288,256]{3,2,1,0:T(8,128)} %state_kernel.3, ...), custom_call_target="tpu_custom_call" | custom-call | tf_op jit(solution)/shard_map/exchange/pallas_call | solution.py:1108
  288.8 14.8 %finish.1 = (f32[2,2,2304,256]{3,2,1,0:T(8,128)}, f32[2,4,256,256]{3,2,1,0:T(8,128)}, f32[2,640,512]{2,1,0:T(8,128)}, f32[2,512,256]{2,1,0:T(8,128)}, f32[27,2,2...) custom-call(f32[3]{0:T(128)} %pad_maximum_fusion.4.scalars, ...), custom_call_target="tpu_custom_call" | custom-call | flops 41943040 | bytes 37748736 | tf_op jit(solution)/shard_map/finish/pallas_call | solution.py:1266
  (46 shorter events, 1.9 us)
Async XLA Ops:
  7.2 281.6 %all-gather.5.cloned.1.call-start = ((), (), s32[]{:S(2)}) async-start(), calls=%async_computation.2 | async-start | bytes 1179648 | tf_op jit(solution)/shard_map/all_gather | solution.py:1445
  8.0 6.7 %copy-start.4 = (f32[128,3,4,16]{0,3,2,1:T(8,128)S(1)}, f32[128,3,4,16]{0,3,2,1:T(8,128)}, u32[]{:S(2)}) copy-start(f32[128,3,4,16]{0,3,2,1:T(8,128)} %param.27) | copy-start | bytes 294916
  8.0 7.1 %copy-start.5 = (f32[128,3,4,16]{0,3,2,1:T(8,128)S(1)}, f32[128,3,4,16]{0,3,2,1:T(8,128)}, u32[]{:S(2)}) copy-start(f32[128,3,4,16]{0,3,2,1:T(8,128)} %param.28) | copy-start | bytes 294916
  15.7 14.4 %collective-permute-start = (f32[32,4,128]{2,0,1:T(8,128)S(1)}, f32[32,4,128]{2,0,1:T(8,128)S(1)}, u32[]{:S(2)}, u32[]{:S(2)}) collective-permute-start(f32[32,4,128]{2,0,1:T(8,128)S(1)} %get-tuple-element.130), channel_id=1, source_target_pairs={{0,3},{1,0},{2,1},{3,2},{4,7},{5,4},{6,5},{7,6},{8,11},{9,8},{10,9... | collective-permute-start | bytes 196616 | tf_op jit(solution)/shard_map/ppermute | solution.py:1367
  18.7 11.4 %collective-permute-start.1 = (f32[32,4,128]{2,0,1:T(8,128)S(1)}, f32[32,4,128]{2,0,1:T(8,128)S(1)}, u32[]{:S(2)}, u32[]{:S(2)}) collective-permute-start(f32[32,4,128]{2,0,1:T(8,128)S(1)} %get-tuple-element.132), channel_id=1, source_target_pairs={{0,2},{1,3},{2,0},{3,1},{4,6},{5,7},{6,4},{7,5},{8,10},{9,11},{10,... | collective-permute-start | bytes 196616 | tf_op jit(solution)/shard_map/ppermute | solution.py:1367
  18.9 6.0 %copy-start.7 = (s32[128]{0:T(128)S(1)}, s32[128]{0:T(128)}, u32[]{:S(2)}) copy-start(s32[128]{0:T(128)} %param.29) | copy-start | bytes 1540
  19.0 6.1 %copy-start.6 = (f32[1000]{0:T(1024)S(1)}, f32[1000]{0:T(1024)}, u32[]{:S(2)}) copy-start(f32[1000]{0:T(1024)} %constant.105) | copy-start | bytes 12004
  19.0 11.2 %collective-permute-start.2 = (f32[32,4,128]{2,0,1:T(8,128)S(1)}, f32[32,4,128]{2,0,1:T(8,128)S(1)}, u32[]{:S(2)}, u32[]{:S(2)}) collective-permute-start(f32[32,4,128]{2,0,1:T(8,128)S(1)} %get-tuple-element.131), channel_id=1, source_target_pairs={{0,1},{1,2},{2,3},{3,0},{4,5},{5,6},{6,7},{7,4},{8,9},{9,10},{10,1... | collective-permute-start | bytes 196616 | tf_op jit(solution)/shard_map/ppermute | solution.py:1367
  19.3 51.7 %all-to-all-start = ((bf16[4,32,64,256]{3,2,1,0:T(8,128)(2,1)}), bf16[4,32,64,256]{3,2,1,0:T(8,128)(2,1)}, u32[]{:S(2)}, u32[]{:S(2)}) async-start(bf16[4,32,64,256]{3,2,1,0:T(8,128)(2,1)} %bitcast.70), calls=%async_computation | async-start | bytes 8388608 | tf_op jit(solution)/shard_map/all_to_all | solution.py:1360
  24.1 264.7 %all-gather.3.cloned.1.call-start = ((), (), s32[]{:S(2)}) async-start(), calls=%async_computation.1 | async-start | bytes 5308416 | tf_op jit(solution)/shard_map/all_gather | solution.py:1444
  31.1 2.7 copy-start
  36.5 1.0 copy-start.1
  36.5 2.5 copy-start.3
  41.5 2.6 copy-start.2
Sparse Core Ops, SparseCore 0:
  9.6 24.5 all-gather.4
  35.9 51.2 all-gather.2
